TPU v7x, 128 devices: a whole 4x4x4 slice. The times are simulated.
128 devices in a mesh: dp: 4 (over z), context: 4 (over y), tensor: 8 (over x, core).
Axes of the slice: x: 4, y: 4, z: 4, core: 2. Of those that a mesh axis runs over, the one named last changes fastest.
Arguments:
- inputs: bfloat16 [8192, 5376], P(('dp', 'context')), may hold values from -8 to 8
- queries: bfloat16 [8192, 2048], P(('dp', 'context'), 'tensor'), may hold values from -8 to 8
- key_states: bfloat16 [8192, 1024], P(('dp', 'context'), 'tensor'), may hold values from -8 to 8
- value_states: bfloat16 [8192, 1024], P(('dp', 'context'), 'tensor'), may hold values from -6 to 6
- out_grad: bfloat16 [8192, 5376], P(('dp', 'context')), may hold values from -8 to 8
- positions: int32 [8192], P(('dp', 'context')), may hold values from 0 to 10239, as said below
- w_query: bfloat16 [5376, 2048], P(None, 'tensor'), may hold values from -0.078125 to 0.078125
- w_key: bfloat16 [5376, 1024], P(None, 'tensor'), may hold values from -0.078125 to 0.078125
- w_value: bfloat16 [5376, 1024], P(None, 'tensor'), may hold values from -0.078125 to 0.078125
- w_output: bfloat16 [5376, 2048], P(None, 'tensor'), may hold values from -0.125 to 0.125
Outputs:
- input_grad: bfloat16 [8192, 5376], P(('dp', 'context', 'tensor'))
- grad_query: float32 [5376, 2048], P(('dp', 'context'), 'tensor')
- grad_key: float32 [5376, 1024], P(('dp', 'context'), 'tensor')
- grad_value: float32 [5376, 1024], P(('dp', 'context'), 'tensor')
- grad_output: float32 [5376, 2048], P(('dp', 'context'), 'tensor')
Inputs may be any that keep to these rules, and one draw needn't show every extreme that they name: Within a document positions rise by one from token to token; a position of 0 starts a new document; the first document of each replica's 2048 tokens may have begun before them.
All inputs are finite; a program needn't handle non-finite values.
Results may differ from a plain program's by a relative error of at most 0.02.
Values may be sent and summed in bfloat16 or wider, within the bound.
A program may use at most 128 MiB of HBM per device.

v0:
```python
import jax
import jax.numpy as jnp
from jax import lax
from jax.sharding import PartitionSpec as P

HD = 128
W = 1024
QSCALAR = 168


def rotate_back(grads, places):
    count = grads.shape[0]
    half = HD // 2
    index = jnp.arange(half, dtype=jnp.float32)
    freq = jnp.power(jnp.float32(10000.0), index * (-2.0 / HD))
    angle = places.astype(jnp.float32)[:, None] * freq[None, :]
    cosine = jnp.cos(angle)[:, None, :]
    sine = jnp.sin(angle)[:, None, :]
    split = grads.reshape(count, -1, 2, half)
    first = split[:, :, 0, :]
    second = split[:, :, 1, :]
    upper = first * cosine + second * sine
    lower = second * cosine - first * sine
    return jnp.stack([upper, lower], axis=2).reshape(count, -1)


def contract_rows(left, right):
    return lax.dot_general(
        left, right, (((0,), (0,)), ((), ())), preferred_element_type=jnp.float32
    )


def contract_cols(left, right):
    return lax.dot_general(
        left, right, (((1,), (1,)), ((), ())), preferred_element_type=jnp.float32
    )


def on_device(
    inputs,
    queries,
    key_states,
    value_states,
    out_grad,
    positions,
    w_query,
    w_key,
    w_value,
    w_output,
):
    count = queries.shape[0]
    head_cols = queries.shape[1]
    kv_cols = key_states.shape[1]
    kv_here = kv_cols // HD
    group = head_cols // kv_cols
    scale = QSCALAR ** (-0.5)
    block = lax.axis_index("context")
    blocks = lax.axis_size("context")
    reach = min((W + count - 2) // count, blocks - 1)
    span = (reach + 1) * count
    whole_keys, whole_values = (
        lax.all_gather(key_states, "context", axis=0, tiled=True),
        lax.all_gather(value_states, "context", axis=0, tiled=True),
    )
    padding = jnp.zeros((reach * count, kv_cols), jnp.bfloat16)
    band_keys = lax.dynamic_slice_in_dim(
        jnp.concatenate([padding, whole_keys], axis=0), block * count, span, 0
    )
    band_values = lax.dynamic_slice_in_dim(
        jnp.concatenate([padding, whole_values], axis=0), block * count, span, 0
    )
    query_index = block * count + jnp.arange(count, dtype=jnp.int32)
    key_index = (block - reach) * count + jnp.arange(span, dtype=jnp.int32)
    doc_start = query_index - positions
    allowed = (key_index[None, :] <= query_index[:, None]) & (
        query_index[:, None] - key_index[None, :] < W
    )
    allowed = allowed & (key_index[None, :] >= doc_start[:, None]) & (key_index[None, :] >= 0)
    query_heads = queries.reshape(count, kv_here, group, HD)
    key_heads = band_keys.reshape(span, kv_here, HD)
    value_heads = band_values.reshape(span, kv_here, HD)
    scores = (
        jnp.einsum("qhgd,khd->hgqk", query_heads, key_heads, preferred_element_type=jnp.float32)
        * scale
    )
    scores = jnp.where(allowed, scores, -1e30)
    top = jnp.max(scores, axis=-1, keepdims=True)
    weights = jnp.exp(scores - top)
    probs = weights / jnp.sum(weights, axis=-1, keepdims=True)
    probs_half = probs.astype(jnp.bfloat16)
    attn = jnp.einsum(
        "hgqk,khd->qhgd", probs_half, value_heads, preferred_element_type=jnp.float32
    ).astype(jnp.bfloat16)
    attn_flat = attn.reshape(count, head_cols)
    dattn = jnp.dot(out_grad, w_output, preferred_element_type=jnp.float32).astype(jnp.bfloat16)
    dattn_heads = dattn.reshape(count, kv_here, group, HD)
    dprobs = jnp.einsum(
        "qhgd,khd->hgqk", dattn_heads, value_heads, preferred_element_type=jnp.float32
    )
    delta = jnp.sum(dattn_heads.astype(jnp.float32) * attn.astype(jnp.float32), axis=-1)
    delta = jnp.transpose(delta, (1, 2, 0))[..., None]
    dscores = (probs * (dprobs - delta) * scale).astype(jnp.bfloat16)
    query_grad = jnp.einsum(
        "hgqk,khd->qhgd", dscores, key_heads, preferred_element_type=jnp.float32
    ).reshape(count, head_cols)
    band_key_grad = jnp.einsum(
        "hgqk,qhgd->khd", dscores, query_heads, preferred_element_type=jnp.float32
    ).reshape(span, kv_cols)
    band_value_grad = jnp.einsum(
        "hgqk,qhgd->khd", probs_half, dattn_heads, preferred_element_type=jnp.float32
    ).reshape(span, kv_cols)
    seg_len = blocks * count
    empty = jnp.zeros((seg_len + reach * count, kv_cols), jnp.float32)
    full_keys = lax.dynamic_update_slice_in_dim(empty, band_key_grad, block * count, 0)[
        reach * count :
    ]
    full_values = lax.dynamic_update_slice_in_dim(empty, band_value_grad, block * count, 0)[
        reach * count :
    ]
    key_grad, value_grad = (
        lax.psum_scatter(full_keys, "context", scatter_dimension=0, tiled=True),
        lax.psum_scatter(full_values, "context", scatter_dimension=0, tiled=True),
    )
    query_lin = rotate_back(query_grad, positions).astype(jnp.bfloat16)
    key_lin = rotate_back(key_grad, positions).astype(jnp.bfloat16)
    value_half = value_grad.astype(jnp.bfloat16)
    total = contract_cols(query_lin, w_query)
    total = total + contract_cols(key_lin, w_key)
    total = total + contract_cols(value_half, w_value)
    input_grad = lax.psum_scatter(total, "tensor", scatter_dimension=0, tiled=True).astype(
        jnp.bfloat16
    )
    terms = (
        contract_rows(inputs, query_lin),
        contract_rows(inputs, key_lin),
        contract_rows(inputs, value_half),
        contract_rows(out_grad, attn_flat),
    )
    summed = (
        lax.psum_scatter(
            terms[0].astype(jnp.bfloat16), ("dp", "context"), scatter_dimension=0, tiled=True
        ).astype(jnp.float32),
        lax.psum_scatter(
            terms[1].astype(jnp.bfloat16), ("dp", "context"), scatter_dimension=0, tiled=True
        ).astype(jnp.float32),
        lax.psum_scatter(
            terms[2].astype(jnp.bfloat16), ("dp", "context"), scatter_dimension=0, tiled=True
        ).astype(jnp.float32),
        lax.psum_scatter(
            terms[3].astype(jnp.bfloat16), ("dp", "context"), scatter_dimension=0, tiled=True
        ).astype(jnp.float32),
    )
    return (input_grad, summed[0], summed[1], summed[2], summed[3])


def solution(mesh):
    return jax.shard_map(
        on_device,
        mesh=mesh,
        in_specs=(
            P(("dp", "context"), None),
            P(("dp", "context"), "tensor"),
            P(("dp", "context"), "tensor"),
            P(("dp", "context"), "tensor"),
            P(("dp", "context"), None),
            P(("dp", "context")),
            P(None, "tensor"),
            P(None, "tensor"),
            P(None, "tensor"),
            P(None, "tensor"),
        ),
        out_specs=(
            P(("dp", "context", "tensor"), None),
            P(("dp", "context"), "tensor"),
            P(("dp", "context"), "tensor"),
            P(("dp", "context"), "tensor"),
            P(("dp", "context"), "tensor"),
        ),
        check_vma=False,
    )
```

profile of v0, /device:TPU:0, one launch (start us, length us, event | category | flops | bytes accessed | tf_op | source)
XLA Modules:
  0.0 441.2 jit_solution(8427026727097141793)
XLA Ops:
  7.8 1.4 fusion.64
  9.3 15.2 %all_gather.6 = bf16[2048,128]{1,0:T(8,128)(2,1)} all-gather(bf16[512,128]{1,0:T(8,128)(2,1)} %param.12), channel_id=1, replica_groups=mesh['dp'=4,'context'=4,'tensor'=8] {'context'}, dimensions={0}, use_global_device_ids=true | all-gather | bytes 655360 | tf_op jit(solution)/shard_map/all_gather | solution.py:62
  24.5 13.7 %all_gather.7 = bf16[2048,128]{1,0:T(8,128)(2,1)} all-gather(bf16[512,128]{1,0:T(8,128)(2,1)} %param.13), channel_id=1, replica_groups=mesh['dp'=4,'context'=4,'tensor'=8] {'context'}, dimensions={0}, use_global_device_ids=true | all-gather | bytes 655360 | tf_op jit(solution)/shard_map/all_gather | solution.py:63
  38.2 2.3 fusion.17
  40.5 2.5 fusion.9
  43.0 1.5 fusion.8
  44.5 2.3 copy-done.8
  46.9 1.6 convolution_convert_fusion.4
  48.5 3.1 fusion.29
  51.6 3.2 fusion.10
  55.0 1.5 copy-done.1
  56.6 1.2 fusion.25
  59.0 4.2 fusion.22
  64.6 19.1 %reduce-scatter.12.cloned.1.call-done = f32[512,128]{0,1:T(8,128)} async-done(((f32[2048,128]{0,1:T(8,128)}), f32[512,128]{0,1:T(8,128)}) %reduce-scatter.12.cloned.1.call-update) | async-done | bytes 262160 | tf_op jit(solution)/shard_map/reduce_scatter | solution.py:121
  83.7 1.5 fusion.47
  85.2 4.6 %fusion.2 = bf16[5376,128]{0,1:T(8,128)(2,1)} fusion(bf16[512,128]{0,1:T(8,128)(2,1)S(1)} %bitcast.146, bf16[512,5376]{1,0:T(8,128)(2,1)} %param.10), kind=kOutput, calls=%fused_computation.7 | convolution fusion | flops 705331200 | bytes 7012352 | tf_op jit(solution)/shard_map/dot_general | solution.py:28
  89.8 19.8 %reduce-scatter.14.cloned.1.call-done = f32[512,128]{0,1:T(8,128)} async-done(((f32[2048,128]{0,1:T(8,128)}), f32[512,128]{0,1:T(8,128)}) %reduce-scatter.14.cloned.1.call-update) | async-done | bytes 262160 | tf_op jit(solution)/shard_map/reduce_scatter | solution.py:122
  109.6 4.6 %fusion.3 = bf16[5376,128]{0,1:T(8,128)(2,1)} fusion(bf16[512,5376]{1,0:T(8,128)(2,1)} %param.10, f32[512,128]{0,1:T(8,128)} %reduce-scatter.14.cloned.1.call-done), kind=kOutput, calls=%fused_computation.8 | convolution fusion | flops 705396736 | bytes 7143424 | tf_op jit(solution)/shard_map/dot_general | solution.py:28
  114.9 2.8 fusion.36
  117.8 5.7 %fusion = bf16[5376,256]{0,1:T(8,128)(2,1)} fusion(bf16[512,256]{0,1:T(8,128)(2,1)S(1)} %bitcast.148, bf16[512,5376]{1,0:T(8,128)(2,1)} %param.10), kind=kOutput, calls=%fused_computation.3 | convolution fusion | flops 1410662400 | bytes 8519680 | tf_op jit(solution)/shard_map/dot_general | solution.py:28
  123.5 4.7 %copy.64 = bf16[5376,256]{1,0:T(8,128)(2,1)} copy(bf16[5376,256]{0,1:T(8,128)(2,1)} %fusion) | data formatting | bytes 5505024
  128.3 5.9 %fusion.1 = bf16[5376,256]{0,1:T(8,128)(2,1)} fusion(bf16[512,256]{0,1:T(8,128)(2,1)S(1)} %bitcast.153, bf16[512,5376]{1,0:T(8,128)(2,1)} %param.14), kind=kOutput, calls=%fused_computation.4 | convolution fusion | flops 1410662400 | bytes 8519680 | tf_op jit(solution)/shard_map/dot_general | solution.py:28
  134.1 4.7 %copy.70 = bf16[5376,256]{1,0:T(8,128)(2,1)} copy(bf16[5376,256]{0,1:T(8,128)(2,1)} %fusion.1) | data formatting | bytes 5505024
  139.1 3.1 fusion.65
  142.2 5.8 %fusion.51 = f32[512,5376]{1,0:T(8,128)} fusion(bf16[5376,128]{1,0:T(8,128)(2,1)S(1)} %copy-done.4, f32[512,128]{0,1:T(8,128)S(1)} %copy-done.5), kind=kOutput, calls=%fused_computation.65 | convolution fusion | flops 704708608 | bytes 12648448 | tf_op jit(solution)/shard_map/dot_general | solution.py:34
  148.0 9.9 %add_add_fusion = f32[512,5376]{1,0:T(8,128)} fusion(f32[512,5376]{1,0:T(8,128)} %fusion.51, f32[512,5376]{1,0:T(8,128)S(1)} %fusion.65, bf16[512,256]{0,1:T(8,128)(2,1)S(1)} %bitcast.149, bf16[5376,256]{1,0:T(8,128)(2,1)S(1)} %copy-done), kind=kOutput, calls=%fused_computation | convolution fusion | flops 1414791168 | bytes 36044800 | tf_op jit(solution)/shard_map/dot_general | solution.py:34
  159.9 48.0 %all-reduce.7.cloned.1.call-done = (bf16[5376,128]{0,1:T(8,128)(2,1)}, bf16[5376,128]{0,1:T(8,128)(2,1)}) async-done(((bf16[5376,128]{0,1:T(8,128)(2,1)}, bf16[5376,128]{0,1:T(8,128)(2,1)}), (bf16[5376,128]{0,1:T(8,128)(2,1)}, bf16[5376,128]{0,1:T(8,128)(2,1)})) %all-reduce.7.cloned.1.call-update) | async-done | bytes 2752528
  207.9 1.1 dynamic-slice_convert_fusion
  210.6 76.3 %reduce-scatter.18.cloned.1.call-done = bf16[336,256]{1,0:T(8,128)(2,1)} async-done(((bf16[5376,256]{1,0:T(8,128)(2,1)}), bf16[336,256]{1,0:T(8,128)(2,1)}) %reduce-scatter.18.cloned.1.call-update) | async-done | bytes 172048
  288.8 76.9 %reduce-scatter.20.cloned.1.call-done = bf16[336,256]{1,0:T(8,128)(2,1)} async-done(((bf16[5376,256]{1,0:T(8,128)(2,1)}), bf16[336,256]{1,0:T(8,128)(2,1)}) %reduce-scatter.20.cloned.1.call-update) | async-done | bytes 172048
  367.7 64.4 %reduce-scatter.16.cloned.1.call-done = f32[64,5376]{1,0:T(8,128)} async-done(((f32[512,5376]{1,0:T(8,128)}), f32[64,5376]{1,0:T(8,128)}) %reduce-scatter.16.cloned.1.call-update) | async-done | bytes 1376272 | tf_op jit(solution)/shard_map/reduce_scatter | solution.py:130
  432.1 2.3 convert_element_type.102
  (58 shorter events, 11.2 us)
Async XLA Ops:
  7.2 140.9 %copy-start = (bf16[5376,256]{1,0:T(8,128)(2,1)S(1)}, bf16[5376,256]{1,0:T(8,128)(2,1)}, u32[]{:S(2)}) copy-start(bf16[5376,256]{1,0:T(8,128)(2,1)} %param.16) | copy-start | bytes 8257540
  7.2 76.5 %reduce-scatter.12.cloned.1.call-start = ((), (), s32[]{:S(2)}) async-start(), calls=%async_computation.5 | async-start | bytes 1310720 | tf_op jit(solution)/shard_map/reduce_scatter | solution.py:121
  38.2 6.3 %slice-start = ((s8[5505024]{0:T(1024)(128)(4,1)}), s8[4194304]{0:T(1024)(128)(4,1)S(1)}, s32[]{:S(2)}) async-start(s8[5505024]{0:T(1024)(128)(4,1)} %bitcast.151), calls=%async_computation.11 | async-start | bytes 8388608
  40.5 4.1 slice-start.1
  43.0 8.6 %copy-start.2 = (f32[1536,512,2]{1,0,2:T(8,128)}, f32[1536,512,2]{1,0,2:T(8,128)S(1)}, u32[]{:S(2)}) copy-start(f32[1536,512,2]{1,0,2:T(8,128)S(1)} %get-tuple-element.31) | copy-start | bytes 18874372
  43.0 3.8 copy-start.8
  46.9 1.6 copy-start.6
  48.5 3.1 copy-start.10
  51.6 4.9 %copy-start.7 = (bf16[512,256]{1,0:T(8,128)(2,1)S(1)}, bf16[512,256]{1,0:T(8,128)(2,1)}, u32[]{:S(2)}) copy-start(bf16[512,256]{1,0:T(8,128)(2,1)} %param.11) | copy-start | bytes 786436
  54.9 1.7 copy-start.1
  58.8 50.8 %reduce-scatter.14.cloned.1.call-start = ((), (), s32[]{:S(2)}) async-start(), calls=%async_computation.6 | async-start | bytes 1310720 | tf_op jit(solution)/shard_map/reduce_scatter | solution.py:122
  64.3 143.6 %all-reduce.7.cloned.1.call-start = ((), (), s32[]{:S(2)}) async-start(), calls=%async_computation.10 | async-start | bytes 5505024
  89.8 25.1 %copy-start.3 = (bf16[2048,128]{1,0:T(8,128)(2,1)S(1)}, bf16[2048,128]{1,0:T(8,128)(2,1)}, u32[]{:S(2)}) copy-start(bf16[2048,128]{1,0:T(8,128)(2,1)} %all_gather.6) | copy-start | bytes 1572868
  114.3 172.6 %reduce-scatter.18.cloned.1.call-start = ((), (), s32[]{:S(2)}) async-start(), calls=%async_computation.8 | async-start | bytes 2924544
  123.5 4.7 %copy-start.9 = (bf16[128,2,512]{2,0,1:T(8,128)(2,1)S(1)}, bf16[128,2,512]{2,0,1:T(8,128)(2,1)}, u32[]{:S(2)}) copy-start(bf16[128,2,512]{2,0,1:T(8,128)(2,1)} %get-tuple-element.33) | copy-start | bytes 786436
  128.2 237.5 %reduce-scatter.20.cloned.1.call-start = ((), (), s32[]{:S(2)}) async-start(), calls=%async_computation.9 | async-start | bytes 2924544
  138.8 3.4 copy-start.5
  138.8 293.2 %reduce-scatter.16.cloned.1.call-start = ((), (), s32[]{:S(2)}) async-start(), calls=%async_computation.7 | async-start | bytes 12386304 | tf_op jit(solution)/shard_map/reduce_scatter | solution.py:130
  139.1 3.1 copy-start.4
  158.0 0.7 copy-start.11
Sparse Core Ops, SparseCore 0:
  58.9 24.6 reduce-scatter.11
  86.1 23.4 reduce-scatter.13
  114.4 93.4 all-reduce.6
  211.1 75.7 reduce-scatter.17
  290.0 75.6 reduce-scatter.19
  368.0 64.0 reduce-scatter.15
where the time goes:
time: 442 us; the launch traced here: 441 us
  waiting for transfers between devices  305 us (69%)
  matrix products  58.2 us (13%)
  blocking collectives  28.9 us (7%)
  local copies, waits for them, and re-layouts  22.4 us (5%)
  between operations  15 us (3%)
  other arithmetic  11.3 us (3%)
    unnamed x9, waiting for transfers between devices  201 us
    reduce_scatter x1, waiting for transfers between devices, on_device(): lax.psum_scatter(total, 'tensor', scatter_dimension=0, tiled=True)  64.4 us
    dot_general x4, matrix products, contract_rows(): lax.dot_general(left, right, (((0,), (0,)), ((), ())), preferred_element_...  20.8 us
    unnamed x37, local copies, waits for them, and re-layouts  20 us
    reduce_scatter x1, waiting for transfers between devices, on_device(): lax.psum_scatter(full_values, 'context', scatter_dimension=0, tiled=True)  19.8 us
    reduce_scatter x1, waiting for transfers between devices, on_device(): lax.psum_scatter(full_keys, 'context', scatter_dimension=0, tiled=True)  19.1 us
    dot_general x3, matrix products, contract_cols(): lax.dot_general(left, right, (((1,), (1,)), ((), ())), preferred_element_...  18.8 us
    all_gather x1, blocking collectives, on_device(): lax.all_gather(key_states, 'context', axis=0, tiled=True)  15.2 us
  transfers between devices with their start and end apart: 6, of which 6 were waited for; matrix products, arithmetic and copies ran while one was open for 14% of the time, Pallas kernels for 0%

commit v1 on v0

v1 whole, which is shorter than its diff:
```python
import functools

import jax
import jax.numpy as jnp
from jax import lax
from jax.experimental import pallas as pl
from jax.experimental.pallas import tpu as pltpu
from jax.sharding import PartitionSpec as P

HD = 128
W = 1024
QSCALAR = 168
D = 5376
ROWS = 512
TILE = 128
WINDOW = W + TILE
BAND = 3 * ROWS
OWN = D // 16
HALF = D // 2
TOP = 176
CHUNK = 384
F32 = jnp.float32
BF16 = jnp.bfloat16
MESH = pl.DeviceIdType.MESH


def nt(left, right):
    return lax.dot_general(left, right, (((1,), (1,)), ((), ())), preferred_element_type=F32)


def nn(left, right):
    return jnp.dot(left, right, preferred_element_type=F32)


def rotate(grad, cosine, sine):
    return grad * cosine + pltpu.roll(grad, HD // 2, 1) * sine


def attention_kernel(
    q_ref, k_ref, v_ref, dattn_ref, lo_ref, cos_ref, sin_ref,
    attn_ref, qlin_ref, own_ref, away_ref, dkt, dvt,
):
    scale = QSCALAR ** (-0.5)
    dkt[...] = jnp.zeros_like(dkt)
    dvt[...] = jnp.zeros_like(dvt)

    def tile(t, carry):
        base = pl.multiple_of(t * TILE, TILE)
        rows = pl.ds(base, TILE)
        wide = pl.ds(base, WINDOW)
        query = jnp.concatenate([q_ref[rows, :HD], q_ref[rows, HD:]], axis=0)
        dattn = jnp.concatenate([dattn_ref[rows, :HD], dattn_ref[rows, HD:]], axis=0)
        keys = k_ref[wide, :]
        values = v_ref[wide, :]
        low = lo_ref[rows, :] - base
        low = jnp.concatenate([low, low], axis=0)
        row = lax.broadcasted_iota(jnp.int32, (2 * TILE, 1), 0) % TILE
        col = lax.broadcasted_iota(jnp.int32, (2 * TILE, WINDOW), 1)
        allowed = (col >= low) & (col <= row + W)
        scores = jnp.where(allowed, nt(query, keys) * scale, -1e30)
        top = jnp.max(scores, axis=-1, keepdims=True)
        weights = jnp.exp(scores - top)
        probs = weights / jnp.sum(weights, axis=-1, keepdims=True)
        half = probs.astype(BF16)
        attn = nn(half, values).astype(BF16)
        attn_ref[rows, :HD] = attn[:TILE]
        attn_ref[rows, HD:] = attn[TILE:]
        dprobs = nt(dattn, values)
        delta = jnp.sum(dattn.astype(F32) * attn.astype(F32), axis=-1, keepdims=True)
        dscores = (probs * (dprobs - delta) * scale).astype(BF16)
        dq = nn(dscores, keys)
        qlin_ref[rows, :HD] = rotate(dq[:TILE], cos_ref[rows, :], sin_ref[rows, :]).astype(BF16)
        qlin_ref[rows, HD:] = rotate(dq[TILE:], cos_ref[rows, :], sin_ref[rows, :]).astype(BF16)
        dkt[:, wide] += nn(query.T, dscores)
        dvt[:, wide] += nn(dattn.T, half)
        return carry

    lax.fori_loop(0, ROWS // TILE, tile, 0)
    for kind, total in enumerate((dkt, dvt)):
        own_ref[kind] = total[:, 2 * ROWS :].T
        away_ref[0, kind] = total[:, ROWS : 2 * ROWS].T.astype(BF16)
        away_ref[1, kind] = total[:, :ROWS].T.astype(BF16)


def attention(q, k, v, dattn, low, cosine, sine):
    vmem = pl.BlockSpec(memory_space=pltpu.VMEM)
    return pl.pallas_call(
        attention_kernel,
        out_shape=(
            jax.ShapeDtypeStruct((ROWS, 2 * HD), BF16),
            jax.ShapeDtypeStruct((ROWS, 2 * HD), BF16),
            jax.ShapeDtypeStruct((2, ROWS, HD), F32),
            jax.ShapeDtypeStruct((2, 2, ROWS, HD), BF16),
        ),
        in_specs=[vmem] * 7,
        out_specs=(vmem,) * 4,
        scratch_shapes=[pltpu.VMEM((HD, BAND), F32), pltpu.VMEM((HD, BAND), F32)],
        compiler_params=pltpu.CompilerParams(vmem_limit_bytes=40 << 20),
        name="attention",
    )(q, k, v, dattn, low, cosine, sine)


def step(axis, index, delta):
    size = 4
    return {axis: lax.rem(index + delta + size, size)}


def reduce_kernel(
    x_hbm, og_hbm, wq_hbm, wk_hbm, wv_hbm, attn_ref, qlin_ref, kv_ref,
    ig_out, gq_out, gk_out, gv_out, go_out,
    x_buf, og_buf, xt, wq, wk, wv, parts, mids, near, far, ig, pair, xring, load_sem,
    c_send, c_recv, e_send, e_recv, f_send, f_recv, g_send, g_recv,
):
    z = lax.axis_index("dp")
    y = lax.axis_index("context")
    t = lax.axis_index("tensor")
    core = lax.rem(t, 2)
    chip = t // 2
    partner = {"tensor": t + 1 - 2 * core}
    xplus = {"tensor": lax.rem(t + 2, 8)}
    xminus = {"tensor": lax.rem(t + 6, 8)}
    loads = [
        pltpu.make_async_copy(src, dst, load_sem.at[i])
        for i, (src, dst) in enumerate(
            ((og_hbm, og_buf), (x_hbm, x_buf), (wq_hbm, wq), (wk_hbm, wk), (wv_hbm, wv))
        )
    ]
    for load in loads:
        load.start()
    barrier = pltpu.get_barrier_semaphore()
    ids = [step("dp", z, 1), step("dp", z, -1), step("context", y, 1), step("context", y, -1)]
    for device in ids + [xplus, xminus, partner]:
        pl.semaphore_signal(barrier, inc=1, device_id=device, device_id_type=MESH)
    pl.semaphore_wait(barrier, 7)

    lines = (("dp", z, "context", y), ("context", y, "dp", z))

    def remote(src, dst, send, recv, device):
        return pltpu.make_async_remote_copy(
            src_ref=src, dst_ref=dst, send_sem=send, recv_sem=recv,
            device_id=device, device_id_type=MESH,
        )

    @functools.cache
    def outer(r, kind):
        axis, me, _, _ = lines[kind]
        there = 4 * lax.rem(me + 2, 4)
        after = 4 * lax.rem(me + 1, 4)
        before = 4 * lax.rem(me + 3, 4)
        up, down = step(axis, me, 1), step(axis, me, -1)
        part = parts.at[r, kind]
        plan = (
            (there, up), (there + 2, down), (after + 2, up), (before, down),
            (after, up), (before + 2, down),
        )
        return [
            remote(
                part.at[pl.ds(start, 2)], near.at[r, kind, n],
                c_send.at[r, kind, n], c_recv.at[r, kind, n], device,
            )
            for n, (start, device) in enumerate(plan)
        ]

    @functools.cache
    def inner(r, kind):
        _, _, axis, me = lines[kind]
        there = lax.rem(me + 2, 4)
        after = lax.rem(me + 1, 4)
        before = lax.rem(me + 3, 4)
        up, down = step(axis, me, 1), step(axis, me, -1)
        upper, lower = pl.ds(0, TOP), pl.ds(TOP, OWN - TOP)
        mid = mids.at[r, kind]
        plan = (
            (there, upper, up), (there, lower, down), (after, lower, up), (before, upper, down),
            (after, upper, up), (before, lower, down),
        )
        return [
            remote(
                mid.at[block, rows], far.at[r, kind, n, pl.ds(0, rows.size)],
                e_send.at[r, kind, n], e_recv.at[r, kind, n], device,
            )
            for n, (block, rows, device) in enumerate(plan)
        ]

    def transpose(src):
        def body(i, carry):
            lanes = pl.ds(pl.multiple_of(i * 128, 128), 128)
            xt[lanes, :] = src[:, lanes].T
            return carry

        lax.fori_loop(0, D // 128, body, 0)

    def multiply(r, right_ref):
        right = right_ref[...]

        def body(o, carry):
            rows = pl.ds(pl.multiple_of(o * OWN, 16), OWN)
            product = nn(xt[rows, :], right).astype(BF16)
            parts[r, 0, o] = product[:, :HD]
            parts[r, 1, lax.rem(o, 4) * 4 + o // 4] = product[:, HD:]
            return carry

        lax.fori_loop(0, 16, body, 0)

    def outer_first(r):
        copies = [outer(r, kind) for kind in range(2)]
        for n in range(4):
            for kind in range(2):
                copies[kind][n].start()

    def outer_second(r):
        for kind in range(2):
            me = lines[kind][1]
            after = 4 * lax.rem(me + 1, 4)
            before = 4 * lax.rem(me + 3, 4)
            copies = outer(r, kind)
            for n, start in ((0, after), (1, before + 2)):
                copies[n].wait_recv()
                where = pl.ds(start, 2)
                parts[r, kind, where] = (
                    parts[r, kind, where].astype(F32) + near[r, kind, n].astype(F32)
                ).astype(BF16)
                copies[4 + n].start()

    outs = ((go_out, go_out), (gq_out, gq_out), (gk_out, gv_out))

    def target(r, kind):
        out = outs[r][kind]
        lanes = pl.ds(HD * kind, HD) if r < 2 else pl.ds(0, HD)
        return out, lanes

    def outer_sum(r, kind, block):
        me = lines[kind][1]
        own = parts[r, kind, 4 * me + block].astype(F32)
        first, second = (4, 3) if block < 2 else (2, 5)
        within = block % 2
        return (
            own + near[r, kind, first, within].astype(F32)
            + near[r, kind, second, within].astype(F32)
        )

    def inner_first(r):
        for kind in range(2):
            copies = outer(r, kind)
            for n in (2, 3, 4, 5):
                copies[n].wait_recv()
            for block in range(4):
                mids[r, kind, block] = outer_sum(r, kind, block)[...].astype(BF16)
            sends = inner(r, kind)
            for n in range(4):
                sends[n].start()

    def inner_second(r):
        for kind in range(2):
            me = lines[kind][3]
            after = lax.rem(me + 1, 4)
            before = lax.rem(me + 3, 4)
            copies = inner(r, kind)
            for n, block, rows in (
                (0, after, pl.ds(0, TOP)), (1, before, pl.ds(TOP, OWN - TOP)),
            ):
                copies[n].wait_recv()
                mids[r, kind, block, rows] = (
                    mids[r, kind, block, rows].astype(F32)
                    + far[r, kind, n, pl.ds(0, rows.size)].astype(F32)
                ).astype(BF16)
                copies[4 + n].start()

    def inner_last(r):
        for kind in range(2):
            me = lines[kind][3]
            copies = inner(r, kind)
            for n in (2, 3, 4, 5):
                copies[n].wait_recv()
            out, lanes = target(r, kind)
            for rows, first, second in (
                (pl.ds(0, TOP), 4, 3), (pl.ds(TOP, OWN - TOP), 2, 5),
            ):
                size = pl.ds(0, rows.size)
                out[rows, lanes] = (
                    mids[r, kind, me, rows].astype(F32)
                    + far[r, kind, first, size].astype(F32)
                    + far[r, kind, second, size].astype(F32)
                )

    there, after, before = lax.rem(chip + 2, 4), lax.rem(chip + 1, 4), lax.rem(chip + 3, 4)

    @functools.cache
    def pair_copies():
        return [
            remote(
                ig.at[1 - core, block], pair.at[block], f_send.at[n], f_recv.at[n], partner
            )
            for n, block in enumerate((there, after, before, chip))
        ]

    @functools.cache
    def ring_copies():
        mine = ig.at[core]
        plan = (
            (there, 0, xplus), (there, 1, xminus), (after, 1, xplus), (before, 0, xminus),
            (after, 0, xplus), (before, 1, xminus),
        )
        return [
            remote(mine.at[block, h], xring.at[n], g_send.at[n], g_recv.at[n], device)
            for n, (block, h, device) in enumerate(plan)
        ]

    def input_multiply():
        query, key, value = qlin_ref[...], kv_ref[:, :HD], kv_ref[:, HD:]
        for h in range(2):
            def body(i, carry, h=h):
                rows = pl.ds(pl.multiple_of(h * HALF + i * CHUNK, 128), CHUNK)
                lanes = pl.ds(pl.multiple_of(i * CHUNK, 128), CHUNK)
                total = nt(query, wq[rows, :]) + nt(key, wk[rows, :]) + nt(value, wv[rows, :])
                total = total.astype(BF16)
                for o in range(8):
                    ig[o % 2, o // 2, h, :, lanes] = total[64 * o : 64 * o + 64]
                return carry

            lax.fori_loop(0, HALF // CHUNK, body, 0)

    def pair_add():
        copies = pair_copies()
        sends = ring_copies()
        for n, block in enumerate((there, after, before, chip)):
            copies[n].wait_recv()
            for h in range(2):
                ig[core, block, h] = (
                    ig[core, block, h].astype(F32) + pair[block, h].astype(F32)
                ).astype(BF16)
            for m in ((0, 1), (2,), (3,), ())[n]:
                sends[m].start()

    def ring_second():
        copies = ring_copies()
        for n, block in ((0, after), (1, before)):
            copies[n].wait_recv()
            ig[core, block, n] = (
                ig[core, block, n].astype(F32) + xring[n].astype(F32)
            ).astype(BF16)
            copies[4 + n].start()

    def ring_last():
        copies = ring_copies()
        for n in (2, 3, 4, 5):
            copies[n].wait_recv()
        for h, first, second in ((0, 4, 3), (1, 2, 5)):
            ig_out[:, pl.ds(h * HALF, HALF)] = (
                ig[core, chip, h].astype(F32) + xring[first].astype(F32)
                + xring[second].astype(F32)
            ).astype(BF16)

    loads[0].wait()
    transpose(og_buf)
    multiply(0, attn_ref)
    outer_first(0)
    loads[1].wait()
    transpose(x_buf)
    multiply(1, qlin_ref)
    outer_first(1)
    multiply(2, kv_ref)
    outer_first(2)
    for load in loads[2:]:
        load.wait()
    input_multiply()
    for copy in pair_copies():
        copy.start()
    outer_second(0)
    pair_add()
    outer_second(1)
    inner_first(0)
    outer_second(2)
    ring_second()
    inner_second(0)
    inner_first(1)
    inner_second(1)
    inner_last(0)
    inner_first(2)
    inner_second(2)
    ring_last()
    inner_last(1)
    inner_last(2)
    for r in range(3):
        for kind in range(2):
            for copy in outer(r, kind) + inner(r, kind):
                copy.wait_send()
    for copy in pair_copies() + ring_copies():
        copy.wait_send()


def reduce_all(x, og, wq, wk, wv, attn, qlin, kv):
    vmem = pl.BlockSpec(memory_space=pltpu.VMEM)
    anywhere = pl.BlockSpec(memory_space=pl.ANY)
    dma = pltpu.SemaphoreType.DMA
    return pl.pallas_call(
        reduce_kernel,
        out_shape=(
            jax.ShapeDtypeStruct((64, D), BF16),
            jax.ShapeDtypeStruct((OWN, 2 * HD), F32),
            jax.ShapeDtypeStruct((OWN, HD), F32),
            jax.ShapeDtypeStruct((OWN, HD), F32),
            jax.ShapeDtypeStruct((OWN, 2 * HD), F32),
        ),
        in_specs=[anywhere] * 5 + [vmem] * 3,
        out_specs=(vmem,) * 5,
        scratch_shapes=[
            pltpu.VMEM((ROWS, D), BF16),
            pltpu.VMEM((ROWS, D), BF16),
            pltpu.VMEM((D, ROWS), BF16),
            pltpu.VMEM((D, 2 * HD), BF16),
            pltpu.VMEM((D, HD), BF16),
            pltpu.VMEM((D, HD), BF16),
            pltpu.VMEM((3, 2, 16, OWN, HD), BF16),
            pltpu.VMEM((3, 2, 4, OWN, HD), BF16),
            pltpu.VMEM((3, 2, 6, 2, OWN, HD), BF16),
            pltpu.VMEM((3, 2, 6, TOP, HD), BF16),
            pltpu.VMEM((2, 4, 2, 64, HALF), BF16),
            pltpu.VMEM((4, 2, 64, HALF), BF16),
            pltpu.VMEM((6, 64, HALF), BF16),
            dma((5,)),
            dma((3, 2, 6)), dma((3, 2, 6)), dma((3, 2, 6)), dma((3, 2, 6)),
            dma((4,)), dma((4,)), dma((6,)), dma((6,)),
        ],
        compiler_params=pltpu.CompilerParams(
            collective_id=0, has_side_effects=True, vmem_limit_bytes=60 << 20
        ),
        name="reduce_all",
    )(x, og, wq, wk, wv, attn, qlin, kv)


def on_device(
    inputs, queries, key_states, value_states, out_grad, positions,
    w_query, w_key, w_value, w_output,
):
    block = lax.axis_index("context")
    kv = jnp.concatenate([key_states, value_states], axis=1)
    ahead = [[(i, i + n) for i in range(4 - n)] for n in (1, 2)]
    back = [[(i + n, i) for i in range(4 - n)] for n in (1, 2)]
    middle = lax.ppermute(kv, "context", ahead[0])
    oldest = lax.ppermute(kv, "context", ahead[1])
    dattn = jnp.dot(out_grad, w_output, preferred_element_type=F32).astype(BF16)
    band = jnp.concatenate([oldest, middle, kv], axis=0)

    row = jnp.arange(ROWS, dtype=jnp.int32)
    index = block * ROWS + row
    low = jnp.maximum(jnp.maximum(index - (W - 1), index - positions), 0) - (block - 2) * ROWS
    order = jnp.arange(HD // 2, dtype=F32)
    freq = jnp.power(F32(10000.0), order * (-2.0 / HD))
    angle = positions.astype(F32)[:, None] * freq[None, :]
    cosine, sine = jnp.cos(angle), jnp.sin(angle)
    cosine = jnp.concatenate([cosine, cosine], axis=1)
    sine = jnp.concatenate([sine, -sine], axis=1)

    attn, qlin, own, away = attention(
        queries, band[:, :HD], band[:, HD:], dattn, low[:, None], cosine, sine
    )
    near = lax.ppermute(away[0], "context", back[0])
    far = lax.ppermute(away[1], "context", back[1])
    total = own + near.astype(F32) + far.astype(F32)
    key_grad = total[0]
    rolled = jnp.concatenate([key_grad[:, HD // 2 :], key_grad[:, : HD // 2]], axis=1)
    key_lin = (key_grad * cosine + rolled * sine).astype(BF16)
    kv_lin = jnp.concatenate([key_lin, total[1].astype(BF16)], axis=1)
    return reduce_all(inputs, out_grad, w_query, w_key, w_value, attn, qlin, kv_lin)


def solution(mesh):
    rows = ("dp", "context")
    return jax.shard_map(
        on_device,
        mesh=mesh,
        in_specs=(
            P(rows, None), P(rows, "tensor"), P(rows, "tensor"), P(rows, "tensor"),
            P(rows, None), P(rows), P(None, "tensor"), P(None, "tensor"),
            P(None, "tensor"), P(None, "tensor"),
        ),
        out_specs=(
            P(("dp", "context", "tensor"), None), P(rows, "tensor"), P(rows, "tensor"),
            P(rows, "tensor"), P(rows, "tensor"),
        ),
        check_vma=False,
    )
```

time: 442 us -> 114 us (0.26)
  waiting for transfers between devices: 305 us -> 9.58 us
  Pallas kernels: 0 us -> 72.6 us
  matrix products: 58.2 us -> 4.15 us
  blocking collectives: 28.9 us -> 0 us
  between operations: 15 us -> 0.85 us
  local copies, waits for them, and re-layouts: 22.4 us -> 10.1 us
  starting transfers between devices: 0.65 us -> 11.7 us
  other arithmetic: 11.3 us -> 3.99 us
    unnamed x9 -> x0, waiting for transfers between devices: 201 us -> none
    reduce_scatter x3 -> x0, waiting for transfers between devices: 103 us -> none  [the longest x1 64.4 us: on_device(): lax.psum_scatter(total, 'tensor', scatter_dimension=0, tiled=True)]
    pallas_call x0 -> x2, Pallas kernels: none -> 72.6 us  [the longest x1 65.9 us: reduce_all(): pl.pallas_call(reduce_kernel, out_shape=(jax.ShapeDtypeStruct((64, D), BF...]
    dot_general x14 -> x1, matrix products: 58.2 us -> 4.15 us  [on_device(): dattn = jnp.dot(out_grad, w_output, preferred_element_type=F32).astype(BF16)]
    all_gather x2 -> x0, blocking collectives: 28.9 us -> none  [the longest x1 15.2 us: on_device(): lax.all_gather(key_states, 'context', axis=0, tiled=True)]
    ppermute x0 -> x4, starting transfers between devices: none -> 11.7 us  [the longest x1 5.5 us: on_device(): oldest = lax.ppermute(kv, 'context', ahead[1])]
    unnamed x37 -> x16, local copies, waits for them, and re-layouts: 20 us -> 8.8 us
    ppermute x0 -> x4, waiting for transfers between devices: none -> 9.58 us  [the longest x1 6.77 us: on_device(): near = lax.ppermute(away[0], 'context', back[0])]
  transfers between devices with their start and end apart: 6 -> 4, of which waited for: 6 -> 2; matrix products, arithmetic and copies ran while one was open for 14% -> 6% of each run, Pallas kernels for 0% -> 0%
where the time goes in v1:
time: 114 us; the launch traced here: 113 us
  Pallas kernels  72.6 us (64%)
  starting transfers between devices  11.7 us (10%)
  local copies, waits for them, and re-layouts  10.1 us (9%)
  waiting for transfers between devices  9.58 us (8%)
  matrix products  4.15 us (4%)
  other arithmetic  3.99 us (4%)
    pallas_call x1, Pallas kernels, reduce_all(): pl.pallas_call(reduce_kernel, out_shape=(jax.ShapeDtypeStruct((64, D), BF...  65.9 us
    unnamed x16, local copies, waits for them, and re-layouts  8.8 us
    ppermute x1, waiting for transfers between devices, on_device(): near = lax.ppermute(away[0], 'context', back[0])  6.77 us
    pallas_call x1, Pallas kernels, attention(): pl.pallas_call(attention_kernel, out_shape=(jax.ShapeDtypeStruct((ROWS, 2...  6.76 us
    ppermute x1, starting transfers between devices, on_device(): oldest = lax.ppermute(kv, 'context', ahead[1])  5.5 us
    dot_general x1, matrix products, on_device(): dattn = jnp.dot(out_grad, w_output, preferred_element_type=F32).astype(BF16)  4.15 us
    ppermute x1, starting transfers between devices, on_device(): middle = lax.ppermute(kv, 'context', ahead[0])  3.61 us
    ppermute x1, waiting for transfers between devices, on_device(): far = lax.ppermute(away[1], 'context', back[1])  2.8 us
  transfers between devices with their start and end apart: 4, of which 2 were waited for; matrix products, arithmetic and copies ran while one was open for 6% of the time, Pallas kernels for 0%

profile of v1, /device:TPU:0, one launch (start us, length us, event | category | flops | bytes accessed | tf_op | source)
XLA Modules:
  0.0 113.0 jit_solution(397675398211995739)
XLA Ops:
  0.6 0.0 copy-start
  0.6 1.1 constant_dynamic-update-slice_fusion.1
  1.7 0.9 constant_dynamic-update-slice_fusion
  2.7 3.6 %collective-permute-start.1 = (bf16[512,256]{1,0:T(8,128)(2,1)S(1)}, bf16[512,256]{1,0:T(8,128)(2,1)S(1)}, u32[]{:S(2)}, u32[]{:S(2)}) collective-permute-start(bf16[512,256]{1,0:T(8,128)(2,1)S(1)} %constant_dynamic-update-slice_fusion), channel_id=1, source_target_pairs={{0,8},{8,16},{16,24},{1,9},{9,17},{17,25},{2,10},{10,18},{18,26},{... | collective-permute-start | bytes 786440 | tf_op jit(solution)/shard_map/ppermute | solution.py:440
  6.3 5.5 %collective-permute-start = (bf16[512,256]{1,0:T(8,128)(2,1)S(1)}, bf16[512,256]{1,0:T(8,128)(2,1)}, u32[]{:S(2)}, u32[]{:S(2)}) collective-permute-start(bf16[512,256]{1,0:T(8,128)(2,1)S(1)} %constant_dynamic-update-slice_fusion), channel_id=1, source_target_pairs={{0,16},{8,24},{1,17},{9,25},{2,18},{10,26},{3,19},{11,27},{4,20},{... | collective-permute-start | bytes 786440 | tf_op jit(solution)/shard_map/ppermute | solution.py:441
  11.8 0.8 fusion.6
  12.6 0.1 copy.15.lo_ref
  12.7 4.1 %convolution_convert_fusion.dattn_ref = bf16[512,256]{1,0:T(8,128)(2,1)S(1)} fusion(bf16[512,5376]{1,0:T(8,128)(2,1)} %og_hbm.1, bf16[5376,256]{1,0:T(8,128)(2,1)S(1)} %copy-done), kind=kOutput, calls=%fused_computation | convolution fusion | flops 1409417216 | bytes 8519680 | tf_op jit(solution)/shard_map/dot_general | solution.py:442
  16.9 0.0 copy-start.3
  16.9 1.0 multiply_sine_fusion
  17.9 0.2 pad_maximum_fusion.1
  18.1 0.0 collective-permute-done.1
  18.1 0.0 collective-permute-done
  18.1 1.0 pad_maximum_fusion
  19.1 0.1 fusion.4
  19.2 6.8 %attention.1 = (bf16[512,256]{1,0:T(8,128)(2,1)S(1)}, bf16[512,256]{1,0:T(8,128)(2,1)S(1)}, f32[2,512,128]{2,1,0:T(8,128)S(1)}, bf16[2,2,512,128]{3,2,1,0:T(8,128)(2,1)S(1)}) custom-call(bf16[512,256]{1,0:T(8,128)(2,1)S(1)} %copy-done.3, bf16[1536,128]{1,0:T(8,128)(2,1)S(1)} %get-tuple-element.14.k_ref, bf16[1536,128]{1,0:T(8,128)(2,1)S(1)} %get-tuple-element.13.v_ref, ...), custom_call_target="tpu_custom_call" | custom-call | tf_op jit(solution)/shard_map/attention/pallas_call | solution.py:87
  26.0 0.0 copy-start.1
  26.0 0.0 copy-start.2
  26.0 1.3 %collective-permute-start.2 = (bf16[2,512,128]{2,1,0:T(8,128)(2,1)S(1)}, bf16[2,512,128]{2,1,0:T(8,128)(2,1)S(1)}, u32[]{:S(2)}, u32[]{:S(2)}) collective-permute-start(bf16[2,512,128]{2,1,0:T(8,128)(2,1)S(1)} %get-tuple-element.15), channel_id=1, source_target_pairs={{8,0},{16,8},{24,16},{9,1},{17,9},{25,17},{10,2},{18,10},{26,18},{... | collective-permute-start | bytes 786440 | tf_op jit(solution)/shard_map/ppermute | solution.py:458
  27.3 1.3 %collective-permute-start.3 = (bf16[2,512,128]{2,1,0:T(8,128)(2,1)S(1)}, bf16[2,512,128]{2,1,0:T(8,128)(2,1)S(1)}, u32[]{:S(2)}, u32[]{:S(2)}) collective-permute-start(bf16[2,512,128]{2,1,0:T(8,128)(2,1)S(1)} %get-tuple-element.16), channel_id=1, source_target_pairs={{16,0},{24,8},{17,1},{25,9},{18,2},{26,10},{19,3},{27,11},{20,4},{... | collective-permute-start | bytes 786440 | tf_op jit(solution)/shard_map/ppermute | solution.py:459
  28.6 6.8 %collective-permute-done.2 = bf16[2,512,128]{2,1,0:T(8,128)(2,1)S(1)} collective-permute-done((bf16[2,512,128]{2,1,0:T(8,128)(2,1)S(1)}, bf16[2,512,128]{2,1,0:T(8,128)(2,1)S(1)}, u32[]{:S(2)}, u32[]{:S(2)}) %collective-permute-start.2) | collective-permute-done | bytes 262176 | tf_op jit(solution)/shard_map/ppermute | solution.py:458
  35.4 2.8 %collective-permute-done.3 = bf16[2,512,128]{2,1,0:T(8,128)(2,1)S(1)} collective-permute-done((bf16[2,512,128]{2,1,0:T(8,128)(2,1)S(1)}, bf16[2,512,128]{2,1,0:T(8,128)(2,1)S(1)}, u32[]{:S(2)}, u32[]{:S(2)}) %collective-permute-start.3) | collective-permute-done | bytes 262176 | tf_op jit(solution)/shard_map/ppermute | solution.py:459
  38.2 0.1 convert_add_fusion
  38.3 0.1 fusion.5
  38.5 0.2 fusion.1
  38.7 0.7 pad_maximum_fusion.3.kv_ref
  39.4 65.9 %reduce_all.1 = (bf16[64,5376]{1,0:T(8,128)(2,1)}, f32[336,256]{1,0:T(8,128)}, f32[336,128]{1,0:T(8,128)}, f32[336,128]{1,0:T(8,128)}, f32[336,256]{1,0:T(8,128)}) custom-call(bf16[512,5376]{1,0:T(8,128)(2,1)} %x_hbm.1, bf16[512,5376]{1,0:T(8,128)(2,1)} %og_hbm.1, bf16[5376,256]{1,0:T(8,128)(2,1)} %wq_hbm.1, bf16[5376,128]{1,0:T(8,128)(2,1)} %wk_hbm.1, ...), custom_call_target="tpu_custom_call" | custom-call | tf_op jit(solution)/shard_map/reduce_all/pallas_call | solution.py:396
  105.3 2.0 %copy.22 = bf16[64,5376]{1,0:T(8,128)(2,1)} copy(bf16[64,5376]{1,0:T(8,128)(2,1)} %get-tuple-element.31) | data formatting | bytes 1376256
  107.4 1.7 %copy.23 = f32[336,256]{1,0:T(8,128)} copy(f32[336,256]{1,0:T(8,128)} %get-tuple-element.32) | data formatting | bytes 688128
  109.1 1.6 %copy.24 = f32[336,128]{1,0:T(8,128)} copy(f32[336,128]{1,0:T(8,128)} %get-tuple-element.33) | data formatting | bytes 344064
  110.7 1.6 %copy.25 = f32[336,128]{1,0:T(8,128)} copy(f32[336,128]{1,0:T(8,128)} %get-tuple-element.34) | data formatting | bytes 344064
  112.3 0.7 copy.26
  (10 shorter events, 0.1 us)
Async XLA Ops:
  0.6 12.1 %copy-start = (bf16[5376,256]{1,0:T(8,128)(2,1)S(1)}, bf16[5376,256]{1,0:T(8,128)(2,1)}, u32[]{:S(2)}) copy-start(bf16[5376,256]{1,0:T(8,128)(2,1)} %param.19) | copy-start | bytes 8257540
  2.7 15.4 %collective-permute-start.1 = (bf16[512,256]{1,0:T(8,128)(2,1)S(1)}, bf16[512,256]{1,0:T(8,128)(2,1)S(1)}, u32[]{:S(2)}, u32[]{:S(2)}) collective-permute-start(bf16[512,256]{1,0:T(8,128)(2,1)S(1)} %constant_dynamic-update-slice_fusion), channel_id=1, source_target_pairs={{0,8},{8,16},{16,24},{1,9},{9,17},{17,25},{2,10},{10,18},{18,26},{... | collective-permute-start | bytes 786440 | tf_op jit(solution)/shard_map/ppermute | solution.py:440
  6.3 11.8 %collective-permute-start = (bf16[512,256]{1,0:T(8,128)(2,1)S(1)}, bf16[512,256]{1,0:T(8,128)(2,1)}, u32[]{:S(2)}, u32[]{:S(2)}) collective-permute-start(bf16[512,256]{1,0:T(8,128)(2,1)S(1)} %constant_dynamic-update-slice_fusion), channel_id=1, source_target_pairs={{0,16},{8,24},{1,17},{9,25},{2,18},{10,26},{3,19},{11,27},{4,20},{... | collective-permute-start | bytes 786440 | tf_op jit(solution)/shard_map/ppermute | solution.py:441
  16.9 2.3 %copy-start.3 = (bf16[512,256]{1,0:T(8,128)(2,1)S(1)}, bf16[512,256]{1,0:T(8,128)(2,1)}, u32[]{:S(2)}) copy-start(bf16[512,256]{1,0:T(8,128)(2,1)} %q_ref.1) | copy-start | bytes 786436
  26.0 12.7 %copy-start.1 = (bf16[512,256]{1,0:T(8,128)(2,1)}, bf16[512,256]{1,0:T(8,128)(2,1)S(1)}, u32[]{:S(2)}) copy-start(bf16[512,256]{1,0:T(8,128)(2,1)S(1)} %get-tuple-element.9.attn_ref) | copy-start | bytes 786436
  26.0 12.7 %copy-start.2 = (bf16[512,256]{1,0:T(8,128)(2,1)}, bf16[512,256]{1,0:T(8,128)(2,1)S(1)}, u32[]{:S(2)}) copy-start(bf16[512,256]{1,0:T(8,128)(2,1)S(1)} %get-tuple-element.10.qlin_ref) | copy-start | bytes 786436
  26.0 9.4 %collective-permute-start.2 = (bf16[2,512,128]{2,1,0:T(8,128)(2,1)S(1)}, bf16[2,512,128]{2,1,0:T(8,128)(2,1)S(1)}, u32[]{:S(2)}, u32[]{:S(2)}) collective-permute-start(bf16[2,512,128]{2,1,0:T(8,128)(2,1)S(1)} %get-tuple-element.15), channel_id=1, source_target_pairs={{8,0},{16,8},{24,16},{9,1},{17,9},{25,17},{10,2},{18,10},{26,18},{... | collective-permute-start | bytes 786440 | tf_op jit(solution)/shard_map/ppermute | solution.py:458
  27.3 10.9 %collective-permute-start.3 = (bf16[2,512,128]{2,1,0:T(8,128)(2,1)S(1)}, bf16[2,512,128]{2,1,0:T(8,128)(2,1)S(1)}, u32[]{:S(2)}, u32[]{:S(2)}) collective-permute-start(bf16[2,512,128]{2,1,0:T(8,128)(2,1)S(1)} %get-tuple-element.16), channel_id=1, source_target_pairs={{16,0},{24,8},{17,1},{25,9},{18,2},{26,10},{19,3},{27,11},{20,4},{... | collective-permute-start | bytes 786440 | tf_op jit(solution)/shard_map/ppermute | solution.py:459
  105.3 7.0 %copy-start.4 = (f32[336,256]{1,0:T(8,128)S(1)}, f32[336,256]{1,0:T(8,128)}, u32[]{:S(2)}) copy-start(f32[336,256]{1,0:T(8,128)} %get-tuple-element.35) | copy-start | bytes 1032196

commit v2 on v1

--- a/solution.py
+++ b/solution.py
@@ -18,7 +18,6 @@
 OWN = D // 16
 HALF = D // 2
 TOP = 176
-CHUNK = 384
 F32 = jnp.float32
 BF16 = jnp.bfloat16
 MESH = pl.DeviceIdType.MESH
@@ -36,81 +35,21 @@
     return grad * cosine + pltpu.roll(grad, HD // 2, 1) * sine
 
 
-def attention_kernel(
-    q_ref, k_ref, v_ref, dattn_ref, lo_ref, cos_ref, sin_ref,
-    attn_ref, qlin_ref, own_ref, away_ref, dkt, dvt,
-):
-    scale = QSCALAR ** (-0.5)
-    dkt[...] = jnp.zeros_like(dkt)
-    dvt[...] = jnp.zeros_like(dvt)
-
-    def tile(t, carry):
-        base = pl.multiple_of(t * TILE, TILE)
-        rows = pl.ds(base, TILE)
-        wide = pl.ds(base, WINDOW)
-        query = jnp.concatenate([q_ref[rows, :HD], q_ref[rows, HD:]], axis=0)
-        dattn = jnp.concatenate([dattn_ref[rows, :HD], dattn_ref[rows, HD:]], axis=0)
-        keys = k_ref[wide, :]
-        values = v_ref[wide, :]
-        low = lo_ref[rows, :] - base
-        low = jnp.concatenate([low, low], axis=0)
-        row = lax.broadcasted_iota(jnp.int32, (2 * TILE, 1), 0) % TILE
-        col = lax.broadcasted_iota(jnp.int32, (2 * TILE, WINDOW), 1)
-        allowed = (col >= low) & (col <= row + W)
-        scores = jnp.where(allowed, nt(query, keys) * scale, -1e30)
-        top = jnp.max(scores, axis=-1, keepdims=True)
-        weights = jnp.exp(scores - top)
-        probs = weights / jnp.sum(weights, axis=-1, keepdims=True)
-        half = probs.astype(BF16)
-        attn = nn(half, values).astype(BF16)
-        attn_ref[rows, :HD] = attn[:TILE]
-        attn_ref[rows, HD:] = attn[TILE:]
-        dprobs = nt(dattn, values)
-        delta = jnp.sum(dattn.astype(F32) * attn.astype(F32), axis=-1, keepdims=True)
-        dscores = (probs * (dprobs - delta) * scale).astype(BF16)
-        dq = nn(dscores, keys)
-        qlin_ref[rows, :HD] = rotate(dq[:TILE], cos_ref[rows, :], sin_ref[rows, :]).astype(BF16)
-        qlin_ref[rows, HD:] = rotate(dq[TILE:], cos_ref[rows, :], sin_ref[rows, :]).astype(BF16)
-        dkt[:, wide] += nn(query.T, dscores)
-        dvt[:, wide] += nn(dattn.T, half)
-        return carry
-
-    lax.fori_loop(0, ROWS // TILE, tile, 0)
-    for kind, total in enumerate((dkt, dvt)):
-        own_ref[kind] = total[:, 2 * ROWS :].T
-        away_ref[0, kind] = total[:, ROWS : 2 * ROWS].T.astype(BF16)
-        away_ref[1, kind] = total[:, :ROWS].T.astype(BF16)
-
-
-def attention(q, k, v, dattn, low, cosine, sine):
-    vmem = pl.BlockSpec(memory_space=pltpu.VMEM)
-    return pl.pallas_call(
-        attention_kernel,
-        out_shape=(
-            jax.ShapeDtypeStruct((ROWS, 2 * HD), BF16),
-            jax.ShapeDtypeStruct((ROWS, 2 * HD), BF16),
-            jax.ShapeDtypeStruct((2, ROWS, HD), F32),
-            jax.ShapeDtypeStruct((2, 2, ROWS, HD), BF16),
-        ),
-        in_specs=[vmem] * 7,
-        out_specs=(vmem,) * 4,
-        scratch_shapes=[pltpu.VMEM((HD, BAND), F32), pltpu.VMEM((HD, BAND), F32)],
-        compiler_params=pltpu.CompilerParams(vmem_limit_bytes=40 << 20),
-        name="attention",
-    )(q, k, v, dattn, low, cosine, sine)
-
-
 def step(axis, index, delta):
     size = 4
     return {axis: lax.rem(index + delta + size, size)}
 
 
-def reduce_kernel(
-    x_hbm, og_hbm, wq_hbm, wk_hbm, wv_hbm, attn_ref, qlin_ref, kv_ref,
+def fused_kernel(
+    q_ref, low_ref, cos_ref, sin_ref,
+    k_hbm, v_hbm, x_hbm, og_hbm, wq_hbm, wk_hbm, wv_hbm, wo_hbm,
     ig_out, gq_out, gk_out, gv_out, go_out,
-    x_buf, og_buf, xt, wq, wk, wv, parts, mids, near, far, ig, pair, xring, load_sem,
+    keys, values, relay, act, weights, dattn, attn, lin, probs, dkt, dvt, gout, gin,
+    parts, mids, near, far, ig, pair, xring, load_sem,
+    a_send, a_recv, b_send, b_recv,
     c_send, c_recv, e_send, e_recv, f_send, f_recv, g_send, g_recv,
 ):
+    scale = QSCALAR ** (-0.5)
     z = lax.axis_index("dp")
     y = lax.axis_index("context")
     t = lax.axis_index("tensor")
@@ -119,17 +58,28 @@
     partner = {"tensor": t + 1 - 2 * core}
     xplus = {"tensor": lax.rem(t + 2, 8)}
     xminus = {"tensor": lax.rem(t + 6, 8)}
-    loads = [
-        pltpu.make_async_copy(src, dst, load_sem.at[i])
-        for i, (src, dst) in enumerate(
-            ((og_hbm, og_buf), (x_hbm, x_buf), (wq_hbm, wq), (wk_hbm, wk), (wv_hbm, wv))
+    yplus, yminus = step("context", y, 1), step("context", y, -1)
+    oldest, middle, latest = pl.ds(0, ROWS), pl.ds(ROWS, ROWS), pl.ds(2 * ROWS, ROWS)
+
+    def load(n, src, dst):
+        return pltpu.make_async_copy(src, dst, load_sem.at[n])
+
+    load_og = load(0, og_hbm, act)
+    load_wo = load(1, wo_hbm, weights.at[:, pl.ds(0, 2 * HD)])
+    load_k = load(2, k_hbm, keys.at[latest])
+    load_v = load(3, v_hbm, values.at[latest])
+    load_x = load(4, x_hbm, act)
+    load_w = [
+        load(5 + n, src, weights.at[:, pl.ds(start, width)])
+        for n, (src, start, width) in enumerate(
+            ((wq_hbm, 0, 2 * HD), (wk_hbm, 2 * HD, HD), (wv_hbm, 3 * HD, HD))
         )
     ]
-    for load in loads:
-        load.start()
+    for copy in (load_k, load_v, load_og, load_wo):
+        copy.start()
     barrier = pltpu.get_barrier_semaphore()
-    ids = [step("dp", z, 1), step("dp", z, -1), step("context", y, 1), step("context", y, -1)]
-    for device in ids + [xplus, xminus, partner]:
+    ids = [yplus, yminus, step("dp", z, 1), step("dp", z, -1), xplus, xminus, partner]
+    for device in ids:
         pl.semaphore_signal(barrier, inc=1, device_id=device, device_id_type=MESH)
     pl.semaphore_wait(barrier, 7)
 
@@ -182,34 +132,89 @@
             for n, (block, rows, device) in enumerate(plan)
         ]
 
-    def transpose(src):
+    def ring(n, src, dst, device):
+        return remote(src, dst, a_send.at[n], a_recv.at[n], device)
+
+    ring_kv = (
+        ring(0, k_hbm, keys.at[middle], yplus),
+        ring(1, v_hbm, relay, yminus),
+        ring(2, v_hbm, values.at[middle], yplus),
+        ring(3, keys.at[middle], keys.at[oldest], yplus),
+        ring(4, relay, values.at[oldest], yminus),
+    )
+
+    def back(n, src, dst, device):
+        return remote(gout.at[src] if src < 3 else gin.at[src - 3], gin.at[dst],
+                      b_send.at[n], b_recv.at[n], device)
+
+    ring_back = (
+        back(0, 0, 0, yminus), back(1, 1, 1, yplus), back(2, 2, 2, yminus),
+        back(3, 3, 3, yminus), back(4, 4, 4, yplus),
+    )
+
+    def stacked(ref, rows):
+        return jnp.concatenate([ref[rows, :HD], ref[rows, HD:]], axis=0)
+
+    def forward(i, carry):
+        base = pl.multiple_of(i * TILE, TILE)
+        rows = pl.ds(base, TILE)
+        wide = pl.ds(base, WINDOW)
+        low = low_ref[rows, :] - base
+        low = jnp.concatenate([low, low], axis=0)
+        row = lax.broadcasted_iota(jnp.int32, (2 * TILE, 1), 0) % TILE
+        col = lax.broadcasted_iota(jnp.int32, (2 * TILE, WINDOW), 1)
+        allowed = (col >= low) & (col <= row + W)
+        scores = jnp.where(allowed, nt(stacked(q_ref, rows), keys[wide, :]) * scale, -1e30)
+        top = jnp.max(scores, axis=-1, keepdims=True)
+        raised = jnp.exp(scores - top)
+        prob = raised / jnp.sum(raised, axis=-1, keepdims=True)
+        probs[i] = prob
+        result = nn(prob.astype(BF16), values[wide, :]).astype(BF16)
+        attn[rows, :HD] = result[:TILE]
+        attn[rows, HD:] = result[TILE:]
+        return carry
+
+    def backward(i, carry):
+        base = pl.multiple_of(i * TILE, TILE)
+        rows = pl.ds(base, TILE)
+        wide = pl.ds(base, WINDOW)
+        grad = stacked(dattn, rows)
+        prob = probs[i]
+        dprobs = nt(grad, values[wide, :])
+        delta = jnp.sum(
+            grad.astype(F32) * stacked(attn, rows).astype(F32), axis=-1, keepdims=True
+        )
+        dscores = (prob * (dprobs - delta) * scale).astype(BF16)
+        dq = nn(dscores, keys[wide, :])
+        lin[rows, :HD] = rotate(dq[:TILE], cos_ref[rows, :], sin_ref[rows, :]).astype(BF16)
+        lin[rows, HD : 2 * HD] = rotate(
+            dq[TILE:], cos_ref[rows, :], sin_ref[rows, :]
+        ).astype(BF16)
+        dkt[:, wide] += nn(stacked(q_ref, rows).T, dscores)
+        dvt[:, wide] += nn(grad.T, prob.astype(BF16))
+        return carry
+
+    def multiply(r, right):
         def body(i, carry):
-            lanes = pl.ds(pl.multiple_of(i * 128, 128), 128)
-            xt[lanes, :] = src[:, lanes].T
+            lanes = pl.ds(pl.multiple_of(i * HALF, 128), HALF)
+            product = lax.dot_general(
+                act[:, lanes], right, (((0,), (0,)), ((), ())), preferred_element_type=F32
+            ).astype(BF16)
+            for j in range(8):
+                rows = slice(OWN * j, OWN * j + OWN)
+                parts[r, 0, 8 * i + j] = product[rows, :HD]
+                parts[r, 1, 4 * (j % 4) + 2 * i + j // 4] = product[rows, HD:]
             return carry
 
-        lax.fori_loop(0, D // 128, body, 0)
-
-    def multiply(r, right_ref):
-        right = right_ref[...]
-
-        def body(o, carry):
-            rows = pl.ds(pl.multiple_of(o * OWN, 16), OWN)
-            product = nn(xt[rows, :], right).astype(BF16)
-            parts[r, 0, o] = product[:, :HD]
-            parts[r, 1, lax.rem(o, 4) * 4 + o // 4] = product[:, HD:]
-            return carry
-
-        lax.fori_loop(0, 16, body, 0)
-
-    def outer_first(r):
-        copies = [outer(r, kind) for kind in range(2)]
-        for n in range(4):
-            for kind in range(2):
-                copies[kind][n].start()
-
-    def outer_second(r):
-        for kind in range(2):
+        lax.fori_loop(0, 2, body, 0)
+
+    def outer_first(r, kinds=(0, 1), order=(0, 1, 2, 3)):
+        for n in order:
+            for kind in kinds:
+                outer(r, kind)[n].start()
+
+    def outer_second(r, kinds=(0, 1)):
+        for kind in kinds:
             me = lines[kind][1]
             after = 4 * lax.rem(me + 1, 4)
             before = 4 * lax.rem(me + 3, 4)
@@ -307,18 +312,10 @@
         ]
 
     def input_multiply():
-        query, key, value = qlin_ref[...], kv_ref[:, :HD], kv_ref[:, HD:]
         for h in range(2):
-            def body(i, carry, h=h):
-                rows = pl.ds(pl.multiple_of(h * HALF + i * CHUNK, 128), CHUNK)
-                lanes = pl.ds(pl.multiple_of(i * CHUNK, 128), CHUNK)
-                total = nt(query, wq[rows, :]) + nt(key, wk[rows, :]) + nt(value, wv[rows, :])
-                total = total.astype(BF16)
-                for o in range(8):
-                    ig[o % 2, o // 2, h, :, lanes] = total[64 * o : 64 * o + 64]
-                return carry
-
-            lax.fori_loop(0, HALF // CHUNK, body, 0)
+            total = nt(lin[...], weights[pl.ds(h * HALF, HALF), :]).astype(BF16)
+            for o in range(8):
+                ig[o % 2, o // 2, h] = total[64 * o : 64 * o + 64]
 
     def pair_add():
         copies = pair_copies()
@@ -351,22 +348,59 @@
                 + xring[second].astype(F32)
             ).astype(BF16)
 
-    loads[0].wait()
-    transpose(og_buf)
-    multiply(0, attn_ref)
-    outer_first(0)
-    loads[1].wait()
-    transpose(x_buf)
-    multiply(1, qlin_ref)
-    outer_first(1)
-    multiply(2, kv_ref)
-    outer_first(2)
-    for load in loads[2:]:
-        load.wait()
+    for copy in ring_kv[:3]:
+        copy.start()
+    load_og.wait()
+    load_wo.wait()
+    dattn[...] = nn(act[...], weights[:, : 2 * HD]).astype(BF16)
+    for copy in load_w:
+        copy.start()
+    ring_kv[0].wait_recv()
+    ring_kv[3].start()
+    ring_kv[1].wait_recv()
+    ring_kv[4].start()
+    dkt[...] = jnp.zeros_like(dkt)
+    dvt[...] = jnp.zeros_like(dvt)
+    load_k.wait()
+    load_v.wait()
+    for copy in ring_kv[2:]:
+        copy.wait_recv()
+    lax.fori_loop(0, ROWS // TILE, forward, 0)
+    multiply(0, attn[...])
+    load_x.start()
+    outer_first(0, order=(0, 1))
+    outer_first(0, kinds=(0,), order=(2, 3))
+    lax.fori_loop(0, ROWS // TILE, backward, 0)
+    gout[0] = dkt[:, oldest].astype(BF16)
+    gout[1] = dvt[:, oldest].astype(BF16)
+    gout[2] = dvt[:, middle].astype(BF16)
+    for copy in ring_back[:3]:
+        copy.start()
+    outer_first(0, kinds=(1,), order=(2, 3))
+    load_x.wait()
+    multiply(1, lin[:, : 2 * HD])
+    outer_second(0, kinds=(0,))
+    outer_first(1, kinds=(0,))
+    ring_back[0].wait_recv()
+    gin[0] = (gin[0].astype(F32) + dkt[:, middle]).astype(BF16)
+    ring_back[3].start()
+    ring_back[1].wait_recv()
+    ring_back[4].start()
+    outer_second(0, kinds=(1,))
+    outer_first(1, kinds=(1,))
+    for copy in load_w:
+        copy.wait()
+    for copy in ring_back[2:]:
+        copy.wait_recv()
+    key_grad = (dkt[:, latest] + gin[3].astype(F32)).T
+    value_grad = (dvt[:, latest] + gin[2].astype(F32) + gin[4].astype(F32)).T
+    lin[:, 2 * HD : 3 * HD] = rotate(key_grad, cos_ref[...], sin_ref[...]).astype(BF16)
+    lin[:, 3 * HD :] = value_grad.astype(BF16)
     input_multiply()
     for copy in pair_copies():
         copy.start()
-    outer_second(0)
+    multiply(2, lin[:, 2 * HD :])
+    outer_first(2)
     pair_add()
     outer_second(1)
     inner_first(0)
@@ -381,6 +415,8 @@
     ring_last()
     inner_last(1)
     inner_last(2)
+    for copy in ring_kv + ring_back:
+        copy.wait_send()
     for r in range(3):
         for kind in range(2):
             for copy in outer(r, kind) + inner(r, kind):
@@ -389,28 +425,38 @@
         copy.wait_send()
 
 
-def reduce_all(x, og, wq, wk, wv, attn, qlin, kv):
+OUTS = (
+    jax.ShapeDtypeStruct((64, D), BF16),
+    jax.ShapeDtypeStruct((OWN, 2 * HD), F32),
+    jax.ShapeDtypeStruct((OWN, HD), F32),
+    jax.ShapeDtypeStruct((OWN, HD), F32),
+    jax.ShapeDtypeStruct((OWN, 2 * HD), F32),
+)
+
+
+def fused(*operands):
     vmem = pl.BlockSpec(memory_space=pltpu.VMEM)
     anywhere = pl.BlockSpec(memory_space=pl.ANY)
     dma = pltpu.SemaphoreType.DMA
     return pl.pallas_call(
-        reduce_kernel,
-        out_shape=(
-            jax.ShapeDtypeStruct((64, D), BF16),
-            jax.ShapeDtypeStruct((OWN, 2 * HD), F32),
-            jax.ShapeDtypeStruct((OWN, HD), F32),
-            jax.ShapeDtypeStruct((OWN, HD), F32),
-            jax.ShapeDtypeStruct((OWN, 2 * HD), F32),
-        ),
-        in_specs=[anywhere] * 5 + [vmem] * 3,
+        fused_kernel,
+        out_shape=OUTS,
+        in_specs=[vmem] * 4 + [anywhere] * 8,
         out_specs=(vmem,) * 5,
         scratch_shapes=[
+            pltpu.VMEM((BAND, HD), BF16),
+            pltpu.VMEM((BAND, HD), BF16),
+            pltpu.VMEM((ROWS, HD), BF16),
             pltpu.VMEM((ROWS, D), BF16),
-            pltpu.VMEM((ROWS, D), BF16),
-            pltpu.VMEM((D, ROWS), BF16),
-            pltpu.VMEM((D, 2 * HD), BF16),
-            pltpu.VMEM((D, HD), BF16),
-            pltpu.VMEM((D, HD), BF16),
+            pltpu.VMEM((D, 4 * HD), BF16),
+            pltpu.VMEM((ROWS, 2 * HD), BF16),
+            pltpu.VMEM((ROWS, 2 * HD), BF16),
+            pltpu.VMEM((ROWS, 4 * HD), BF16),
+            pltpu.VMEM((ROWS // TILE, 2 * TILE, WINDOW), F32),
+            pltpu.VMEM((HD, BAND), F32),
+            pltpu.VMEM((HD, BAND), F32),
+            pltpu.VMEM((3, HD, ROWS), BF16),
+            pltpu.VMEM((5, HD, ROWS), BF16),
             pltpu.VMEM((3, 2, 16, OWN, HD), BF16),
             pltpu.VMEM((3, 2, 4, OWN, HD), BF16),
             pltpu.VMEM((3, 2, 6, 2, OWN, HD), BF16),
@@ -418,15 +464,30 @@
             pltpu.VMEM((2, 4, 2, 64, HALF), BF16),
             pltpu.VMEM((4, 2, 64, HALF), BF16),
             pltpu.VMEM((6, 64, HALF), BF16),
-            dma((5,)),
+            dma((8,)),
+            dma((5,)), dma((5,)), dma((5,)), dma((5,)),
             dma((3, 2, 6)), dma((3, 2, 6)), dma((3, 2, 6)), dma((3, 2, 6)),
             dma((4,)), dma((4,)), dma((6,)), dma((6,)),
         ],
         compiler_params=pltpu.CompilerParams(
-            collective_id=0, has_side_effects=True, vmem_limit_bytes=60 << 20
+            collective_id=0, has_side_effects=True, vmem_limit_bytes=66_900_000
         ),
-        name="reduce_all",
-    )(x, og, wq, wk, wv, attn, qlin, kv)
+        name="fused",
+    )(*operands)
+
+
+def finish_kernel(*refs):
+    for src, dst in zip(refs[:5], refs[5:]):
+        dst[...] = src[...]
+
+
+def finish(*results):
+    vmem = pl.BlockSpec(memory_space=pltpu.VMEM)
+    return pl.pallas_call(
+        finish_kernel, out_shape=OUTS, in_specs=[vmem] * 5, out_specs=(vmem,) * 5,
+        compiler_params=pltpu.CompilerParams(vmem_limit_bytes=8 << 20),
+        name="finish",
+    )(*results)
 
 
 def on_device(
@@ -434,14 +495,6 @@
     w_query, w_key, w_value, w_output,
 ):
     block = lax.axis_index("context")
-    kv = jnp.concatenate([key_states, value_states], axis=1)
-    ahead = [[(i, i + n) for i in range(4 - n)] for n in (1, 2)]
-    back = [[(i + n, i) for i in range(4 - n)] for n in (1, 2)]
-    middle = lax.ppermute(kv, "context", ahead[0])
-    oldest = lax.ppermute(kv, "context", ahead[1])
-    dattn = jnp.dot(out_grad, w_output, preferred_element_type=F32).astype(BF16)
-    band = jnp.concatenate([oldest, middle, kv], axis=0)
-
     row = jnp.arange(ROWS, dtype=jnp.int32)
     index = block * ROWS + row
     low = jnp.maximum(jnp.maximum(index - (W - 1), index - positions), 0) - (block - 2) * ROWS
@@ -451,18 +504,12 @@
     cosine, sine = jnp.cos(angle), jnp.sin(angle)
     cosine = jnp.concatenate([cosine, cosine], axis=1)
     sine = jnp.concatenate([sine, -sine], axis=1)
-
-    attn, qlin, own, away = attention(
-        queries, band[:, :HD], band[:, HD:], dattn, low[:, None], cosine, sine
+    return finish(
+        *fused(
+            queries, low[:, None], cosine, sine, key_states, value_states,
+            inputs, out_grad, w_query, w_key, w_value, w_output,
+        )
     )
-    near = lax.ppermute(away[0], "context", back[0])
-    far = lax.ppermute(away[1], "context", back[1])
-    total = own + near.astype(F32) + far.astype(F32)
-    key_grad = total[0]
-    rolled = jnp.concatenate([key_grad[:, HD // 2 :], key_grad[:, : HD // 2]], axis=1)
-    key_lin = (key_grad * cosine + rolled * sine).astype(BF16)
-    kv_lin = jnp.concatenate([key_lin, total[1].astype(BF16)], axis=1)
-    return reduce_all(inputs, out_grad, w_query, w_key, w_value, attn, qlin, kv_lin)
 
 
 def solution(mesh):

time: 114 us -> 93.6 us (0.82)
  starting transfers between devices: 11.7 us -> 0 us
  Pallas kernels: 72.6 us -> 84.1 us
  waiting for transfers between devices: 9.58 us -> 0 us
  local copies, waits for them, and re-layouts: 10.1 us -> 5.74 us
  matrix products: 4.15 us -> 0 us
  other arithmetic: 3.99 us -> 2.77 us
    ppermute x4 -> x0, starting transfers between devices: 11.7 us -> none  [the longest x1 5.5 us: on_device(): oldest = lax.ppermute(kv, 'context', ahead[1])]
    pallas_call x2, Pallas kernels: 72.6 us -> 84.1 us  [the longest x1 82.8 us: fused(): pl.pallas_call(fused_kernel, out_shape=OUTS, in_specs=[vmem] * 4 + [anywh...]
    ppermute x4 -> x0, waiting for transfers between devices: 9.58 us -> none  [the longest x1 6.77 us: on_device(): near = lax.ppermute(away[0], 'context', back[0])]
    dot_general x1 -> x0, matrix products: 4.15 us -> none  [on_device(): dattn = jnp.dot(out_grad, w_output, preferred_element_type=F32).astype(BF16)]
    unnamed x16 -> x10, local copies, waits for them, and re-layouts: 8.8 us -> 4.88 us
    concatenate x2 -> x0, other arithmetic: 1.74 us -> none  [the longest x1 1 us: on_device(): band = jnp.concatenate([oldest, middle, kv], axis=0)]
  transfers between devices with their start and end apart: 4 -> 0, of which waited for: 2 -> 0; matrix products, arithmetic and copies ran while one was open for 6% -> 0% of each run, Pallas kernels for 0% -> 0%
where the time goes in v2:
time: 93.6 us; the launch traced here: 93.3 us
  Pallas kernels  84.1 us (90%)
  local copies, waits for them, and re-layouts  5.74 us (6%)
  other arithmetic  2.77 us (3%)
    pallas_call x1, Pallas kernels, fused(): pl.pallas_call(fused_kernel, out_shape=OUTS, in_specs=[vmem] * 4 + [anywh...  82.8 us
    unnamed x10, local copies, waits for them, and re-layouts  4.88 us

profile of v2, /device:TPU:0, one launch (start us, length us, event | category | flops | bytes accessed | tf_op | source)
XLA Modules:
  0.0 93.3 jit_solution(13500953811360333525)
XLA Ops:
  0.7 0.8 fusion.1
  1.4 0.9 copy.15.low_ref
  2.3 1.0 %multiply_sine_fusion = (f32[512,64]{1,0:T(8,128)S(1)}, f32[512,64]{1,0:T(8,128)S(1)}, f32[512,64]{1,0:T(8,128)S(1)}) fusion(f32[64]{0:T(128)S(1)} %multiply_power_fusion, f32[512]{0:T(512)S(1)} %get-tuple-element.18), kind=kLoop, calls=%fused_computation | loop fusion | flops 65536 | bytes 395520 | tf_op jit(solution)/shard_map/sin | solution.py:504
  3.3 1.0 %pad_maximum_fusion = (f32[512,128]{1,0:T(8,128)}, f32[512,128]{1,0:T(8,128)}) fusion(f32[512,64]{1,0:T(8,128)S(1)} %get-tuple-element.17, f32[512,64]{1,0:T(8,128)S(1)} %get-tuple-element.16, f32[512,64]{1,0:T(8,128)S(1)} %get-tuple-element.15), kind=kLoop, calls=%fused_computation.2 | loop fusion | flops 131072 | bytes 917504 | tf_op jit(solution)/shard_map/concatenate | solution.py:505
  4.3 82.8 %fused.1 = (bf16[64,5376]{1,0:T(8,128)(2,1)}, f32[336,256]{1,0:T(8,128)}, f32[336,128]{1,0:T(8,128)}, f32[336,128]{1,0:T(8,128)}, f32[336,256]{1,0:T(8,128)}) custom-call(bf16[512,256]{1,0:T(8,128)(2,1)} %q_ref.1, s32[512,1]{1,0:T(8,128)} %copy.15.low_ref, f32[512,128]{1,0:T(8,128)} %get-tuple-element.20.cos_ref, f32[512,128]{1,0:T(8,128)} %get-tuple-element.21.sin_ref, ...), custom_call_target="tpu_custom_call" | custom-call | tf_op jit(solution)/shard_map/fused/pallas_call | solution.py:441
  87.1 0.0 copy-start
  87.1 1.1 %copy-done = bf16[64,5376]{1,0:T(8,128)(2,1)S(1)} copy-done((bf16[64,5376]{1,0:T(8,128)(2,1)S(1)}, bf16[64,5376]{1,0:T(8,128)(2,1)}, u32[]{:S(2)}) %copy-start) | copy-done | bytes 688152
  88.2 0.0 copy-start.1
  88.2 1.0 %copy-done.1 = f32[336,256]{1,0:T(8,128)S(1)} copy-done((f32[336,256]{1,0:T(8,128)S(1)}, f32[336,256]{1,0:T(8,128)}, u32[]{:S(2)}) %copy-start.1) | copy-done | bytes 344088
  89.2 0.0 copy-start.2
  89.2 1.0 %copy-done.2 = f32[336,256]{1,0:T(8,128)S(1)} copy-done((f32[336,256]{1,0:T(8,128)S(1)}, f32[336,256]{1,0:T(8,128)}, u32[]{:S(2)}) %copy-start.2) | copy-done | bytes 344088
  90.2 0.0 copy-start.3
  90.2 0.9 copy-done.3
  91.1 0.0 copy-start.4
  91.1 0.9 copy-done.4
  92.0 1.3 %finish.1 = (bf16[64,5376]{1,0:T(8,128)(2,1)}, f32[336,256]{1,0:T(8,128)}, f32[336,128]{1,0:T(8,128)}, f32[336,128]{1,0:T(8,128)}, f32[336,256]{1,0:T(8,128)}) custom-call(bf16[64,5376]{1,0:T(8,128)(2,1)S(1)} %copy-done, f32[336,256]{1,0:T(8,128)S(1)} %copy-done.1, f32[336,128]{1,0:T(8,128)S(1)} %copy-done.3, f32[336,128]{1,0:T(8,128)S(1)} %copy-done.4, ...), custom_call_target="tpu_custom_call" | custom-call | tf_op jit(solution)/shard_map/finish/pallas_call | solution.py:486
  (1 shorter events, 0.0 us)
Async XLA Ops:
  87.1 1.1 %copy-start = (bf16[64,5376]{1,0:T(8,128)(2,1)S(1)}, bf16[64,5376]{1,0:T(8,128)(2,1)}, u32[]{:S(2)}) copy-start(bf16[64,5376]{1,0:T(8,128)(2,1)} %get-tuple-element.10.refs_0_) | copy-start | bytes 2064388
  88.2 1.0 %copy-start.1 = (f32[336,256]{1,0:T(8,128)S(1)}, f32[336,256]{1,0:T(8,128)}, u32[]{:S(2)}) copy-start(f32[336,256]{1,0:T(8,128)} %get-tuple-element.11.refs_1_) | copy-start | bytes 1032196
  89.2 1.0 %copy-start.2 = (f32[336,256]{1,0:T(8,128)S(1)}, f32[336,256]{1,0:T(8,128)}, u32[]{:S(2)}) copy-start(f32[336,256]{1,0:T(8,128)} %get-tuple-element.14.refs_4_) | copy-start | bytes 1032196
  90.2 0.9 copy-start.3
  91.1 0.9 copy-start.4

commit v3 on v2

v3 whole, which is shorter than its diff:
```python
import functools

import jax
import jax.numpy as jnp
import numpy as np
from jax import lax
from jax.experimental import pallas as pl
from jax.experimental.pallas import tpu as pltpu
from jax.sharding import PartitionSpec as P

HD = 128
W = 1024
QSCALAR = 168
D = 5376
ROWS = 512
TILE = 128
WINDOW = W + TILE
BAND = 3 * ROWS
OWN = D // 16
HALF = D // 2
SPAN = 1408
TOP = 176
F32 = jnp.float32
BF16 = jnp.bfloat16
MESH = pl.DeviceIdType.MESH


def nt(left, right):
    return lax.dot_general(left, right, (((1,), (1,)), ((), ())), preferred_element_type=F32)


def nn(left, right):
    return jnp.dot(left, right, preferred_element_type=F32)


def rotate(grad, cosine, sine):
    return grad * cosine + pltpu.roll(grad, HD // 2, 1) * sine


def step(axis, index, delta):
    size = 4
    return {axis: lax.rem(index + delta + size, size)}


def fused_kernel(
    q_ref, k_ref, v_ref, place_ref, freq_ref,
    x_hbm, og_hbm, wq_hbm, wk_hbm, wv_hbm, wo_hbm,
    ig_hbm, gq_hbm, gk_hbm, gv_hbm, go_hbm,
    ig_out, gq_out, gk_out, gv_out, go_out, low_ref, cos_ref, sin_ref,
    keys, values, relay, og, wide_x, wq, wkv, dattn, attn, lin, swap_out, swap_in,
    probs, dkt, dvt, gout, gin, product,
    parts, near, mid_half, mid_full, far_half, far_full, ig, pair, xring, load_sem, out_sem,
    a_send, a_recv, b_send, b_recv, c_send, c_recv, e_send, e_recv,
    f_send, f_recv, g_send, g_recv, h_send, h_recv, l_send, l_recv,
):
    scale = QSCALAR ** (-0.5)
    z = lax.axis_index("dp")
    y = lax.axis_index("context")
    t = lax.axis_index("tensor")
    core = lax.rem(t, 2)
    chip = t // 2
    partner = {"tensor": t + 1 - 2 * core}
    tplus, tminus, tfar = lax.rem(t + 2, 8), lax.rem(t + 6, 8), lax.rem(t + 4, 8)
    xplus, xminus = {"tensor": tplus}, {"tensor": tminus}
    yplus, yminus = step("context", y, 1), step("context", y, -1)
    zplus, zminus, zfar = step("dp", z, 1), step("dp", z, -1), step("dp", z, 2)
    oldest, middle, latest = pl.ds(0, ROWS), pl.ds(ROWS, ROWS), pl.ds(2 * ROWS, ROWS)

    def load(n, src, dst):
        return pltpu.make_async_copy(src, dst, load_sem.at[n])

    def columns(delta):
        there = lax.rem(z + delta, 4)
        return pl.ds(pl.multiple_of(4 * OWN * there - 64 * lax.rem(there, 2), 128), SPAN)

    load_og = load(0, og_hbm, og)
    load_wo = load(1, wo_hbm, wq)
    load_x = load(4, x_hbm.at[:, columns(0)], wide_x.at[0])
    load_wq = load(5, wq_hbm, wq)
    load_wk = load(6, wk_hbm, wkv.at[:, pl.ds(0, HD)])
    load_wv = load(7, wv_hbm, wkv.at[:, pl.ds(HD, HD)])
    barrier = pltpu.get_barrier_semaphore()
    for device in (yplus, yminus, zplus, zminus, zfar, xplus, xminus, partner):
        pl.semaphore_signal(barrier, inc=1, device_id=device, device_id_type=MESH)
    pl.semaphore_wait(barrier, 8)

    lines = (("dp", z, "context", y), ("context", y, "dp", z))

    def remote(src, dst, send, recv, device):
        return pltpu.make_async_remote_copy(
            src_ref=src, dst_ref=dst, send_sem=send, recv_sem=recv,
            device_id=device, device_id_type=MESH,
        )

    def ring(n, src, dst, device):
        return remote(src, dst, a_send.at[n], a_recv.at[n], device)

    ring_kv = (
        ring(0, k_ref, keys.at[middle], yplus),
        ring(1, v_ref, relay, yminus),
        ring(2, v_ref, values.at[middle], yplus),
        ring(3, keys.at[middle], keys.at[oldest], yplus),
        ring(4, relay, values.at[oldest], yminus),
    )

    def back(n, src, dst, device):
        return remote(gout.at[src] if src < 3 else gin.at[src - 3], gin.at[dst],
                      b_send.at[n], b_recv.at[n], device)

    ring_back = (
        back(0, 0, 0, yminus), back(1, 1, 1, yplus), back(2, 2, 2, yminus),
        back(3, 3, 3, yminus), back(4, 4, 4, yplus),
    )

    def eighth(where, start=0, size=64):
        return wide_x.at[pl.ds(1, 3), pl.ds(pl.multiple_of(64 * where + start, 16), size)]

    def move(n, src, dst, device):
        return remote(src, dst, h_send.at[n], h_recv.at[n], device)

    mine = pl.ds(pl.multiple_of(64 * t, 64), 64)
    move_z = [
        move(n, x_hbm.at[mine, columns(delta)], wide_x.at[4 - delta, mine], device)
        for n, (delta, device) in enumerate(((1, zplus), (3, zminus), (2, zfar)))
    ]
    move_x = [
        move(3, eighth(t), eighth(t), xplus),
        move(4, eighth(t), eighth(t), xminus),
        move(5, eighth(tminus, 0, 32), eighth(tminus, 0, 32), xplus),
        move(6, eighth(tplus, 32, 32), eighth(tplus, 32, 32), xminus),
    ]
    move_core = [
        move(7 + n, eighth(where), eighth(where), partner)
        for n, where in enumerate((t, tminus, tplus, tfar))
    ]
    move_w = [
        move(11, wk_hbm, wkv.at[:, pl.ds(2 * HD, HD)], partner),
        move(12, wv_hbm, wkv.at[:, pl.ds(3 * HD, HD)], partner),
    ]
    move_swap = move(13, swap_out, swap_in, partner)

    @functools.cache
    def gather(r):
        first, second = pl.ds(0, ROWS // 2), pl.ds(ROWS // 2, ROWS // 2)
        plan = (
            (lin.at[r, 0], lin.at[r, 3], zplus),
            (lin.at[r, 0], lin.at[r, 1], zminus),
            (lin.at[r, 3, first], lin.at[r, 2, first], zplus),
            (lin.at[r, 1, second], lin.at[r, 2, second], zminus),
        )
        return [
            remote(src, dst, l_send.at[r, n], l_recv.at[r, n], device)
            for n, (src, dst, device) in enumerate(plan)
        ]

    def gather_relay(r):
        for n in range(2):
            gather(r)[n].wait_recv()
            gather(r)[2 + n].start()

    @functools.cache
    def outer(kind):
        axis, me, _, _ = lines[kind]
        there = 4 * lax.rem(me + 2, 4)
        after = 4 * lax.rem(me + 1, 4)
        before = 4 * lax.rem(me + 3, 4)
        up, down = step(axis, me, 1), step(axis, me, -1)
        plan = (
            (there, up), (there + 2, down), (after + 2, up), (before, down),
            (after, up), (before + 2, down),
        )
        return [
            remote(
                parts.at[kind, pl.ds(start, 2)], near.at[kind, n],
                c_send.at[kind, n], c_recv.at[kind, n], device,
            )
            for n, (start, device) in enumerate(plan)
        ]

    upper, lower = pl.ds(0, TOP), pl.ds(TOP, OWN - TOP)
    stages = (
        ("context", y, mid_half.at[0], far_half.at[0]),
        ("dp", z, mid_half.at[1], far_half.at[1]),
        ("context", y, mid_full.at[0], far_full.at[0]),
        ("context", y, mid_full.at[1], far_full.at[1]),
    )

    @functools.cache
    def inner(s):
        axis, me, mid, far = stages[s]
        there = lax.rem(me + 2, 4)
        after = lax.rem(me + 1, 4)
        before = lax.rem(me + 3, 4)
        up, down = step(axis, me, 1), step(axis, me, -1)
        plan = (
            (there, upper, up), (there, lower, down), (after, lower, up), (before, upper, down),
            (after, upper, up), (before, lower, down),
        )
        return [
            remote(
                mid.at[block, rows], far.at[n, pl.ds(0, rows.size)],
                e_send.at[s, n], e_recv.at[s, n], device,
            )
            for n, (block, rows, device) in enumerate(plan)
        ]

    def stacked(ref, rows):
        return jnp.concatenate([ref[rows, :HD], ref[rows, HD:]], axis=0)

    def forward(i, carry):
        base = pl.multiple_of(i * TILE, TILE)
        rows = pl.ds(base, TILE)
        wide = pl.ds(base, WINDOW)
        low = low_ref[rows, :1] - base
        low = jnp.concatenate([low, low], axis=0)
        row = lax.broadcasted_iota(jnp.int32, (2 * TILE, 1), 0) % TILE
        col = lax.broadcasted_iota(jnp.int32, (2 * TILE, WINDOW), 1)
        allowed = (col >= low) & (col <= row + W)
        scores = jnp.where(allowed, nt(stacked(q_ref, rows), keys[wide, :]) * scale, -1e30)
        top = jnp.max(scores, axis=-1, keepdims=True)
        raised = jnp.exp(scores - top)
        prob = raised / jnp.sum(raised, axis=-1, keepdims=True)
        probs[i] = prob
        result = nn(prob.astype(BF16), values[wide, :]).astype(BF16)
        attn[rows, :HD] = result[:TILE]
        attn[rows, HD:] = result[TILE:]
        return carry

    def backward(i, carry):
        base = pl.multiple_of(i * TILE, TILE)
        rows = pl.ds(base, TILE)
        wide = pl.ds(base, WINDOW)
        grad = stacked(dattn, rows)
        prob = probs[i]
        dprobs = nt(grad, values[wide, :])
        delta = jnp.sum(
            grad.astype(F32) * stacked(attn, rows).astype(F32), axis=-1, keepdims=True
        )
        dscores = (prob * (dprobs - delta) * scale).astype(BF16)
        dq = nn(dscores, keys[wide, :])
        lin[0, 0, rows, :HD] = rotate(dq[:TILE], cos_ref[rows, :], sin_ref[rows, :]).astype(BF16)
        lin[0, 0, rows, HD:] = rotate(
            dq[TILE:], cos_ref[rows, :], sin_ref[rows, :]
        ).astype(BF16)
        dkt[:, wide] += nn(stacked(q_ref, rows).T, dscores)
        dvt[:, wide] += nn(grad.T, prob.astype(BF16))
        return carry

    def outer_multiply():
        right = attn[...]

        def body(i, carry):
            lanes = pl.ds(pl.multiple_of(i * HALF, 128), HALF)
            result = lax.dot_general(
                og[:, lanes], right, (((0,), (0,)), ((), ())), preferred_element_type=F32
            ).astype(BF16)
            for j in range(8):
                rows = slice(OWN * j, OWN * j + OWN)
                parts[0, 8 * i + j] = result[rows, :HD]
                parts[1, 4 * (j % 4) + 2 * i + j // 4] = result[rows, HD:]
            return carry

        lax.fori_loop(0, 2, body, 0)

    def outer_first(kinds, order):
        for n in order:
            for kind in kinds:
                outer(kind)[n].start()

    def outer_second(kind):
        me = lines[kind][1]
        after = 4 * lax.rem(me + 1, 4)
        before = 4 * lax.rem(me + 3, 4)
        for n, start in ((0, after), (1, before + 2)):
            outer(kind)[n].wait_recv()
            where = pl.ds(start, 2)
            parts[kind, where] = (
                parts[kind, where].astype(F32) + near[kind, n].astype(F32)
            ).astype(BF16)
            outer(kind)[4 + n].start()

    def inner_start(s):
        for n in range(4):
            inner(s)[n].start()

    def outer_last(kind):
        me = lines[kind][1]
        for n in (2, 3, 4, 5):
            outer(kind)[n].wait_recv()
        for block in range(4):
            first, second = (4, 3) if block < 2 else (2, 5)
            mid_half[kind, block] = (
                parts[kind, 4 * me + block].astype(F32)
                + near[kind, first, block % 2].astype(F32)
                + near[kind, second, block % 2].astype(F32)
            ).astype(BF16)
        inner_start(kind)

    def inner_multiply(r):
        product[...] = jnp.zeros_like(product)

        def body(j, carry):
            product[...] += lax.dot_general(
                wide_x[j], lin[r, j], (((0,), (0,)), ((), ())), preferred_element_type=F32
            )
            return carry

        lax.fori_loop(0, 4, body, 0)
        for block in range(4):
            start = pl.multiple_of(64 * lax.rem(z, 2) + OWN * block, 16)
            mid_full[r, block] = product[pl.ds(start, OWN), :].astype(BF16)
        inner_start(2 + r)

    def inner_second(s):
        _, me, mid, far = stages[s]
        after = lax.rem(me + 1, 4)
        before = lax.rem(me + 3, 4)
        for n, block, rows in ((0, after, upper), (1, before, lower)):
            inner(s)[n].wait_recv()
            mid[block, rows] = (
                mid[block, rows].astype(F32) + far[n, pl.ds(0, rows.size)].astype(F32)
            ).astype(BF16)
            inner(s)[4 + n].start()

    def inner_last(s, outs):
        _, me, mid, far = stages[s]
        for n in (2, 3, 4, 5):
            inner(s)[n].wait_recv()
        for rows, first, second in ((upper, 4, 3), (lower, 2, 5)):
            size = pl.ds(0, rows.size)
            total = (
                mid[me, rows].astype(F32) + far[first, size].astype(F32)
                + far[second, size].astype(F32)
            )
            for out, source, lanes in outs:
                out[rows, lanes] = total[:, source]

    there, after, before = lax.rem(chip + 2, 4), lax.rem(chip + 1, 4), lax.rem(chip + 3, 4)
    pair_copies = [
        remote(ig.at[1 - core, block], pair.at[block], f_send.at[n], f_recv.at[n], partner)
        for n, block in enumerate((there, after, before, chip))
    ]
    ring_x = [
        remote(ig.at[core, block, h], xring.at[n], g_send.at[n], g_recv.at[n], device)
        for n, (block, h, device) in enumerate((
            (there, 0, xplus), (there, 1, xminus), (after, 1, xplus), (before, 0, xminus),
            (after, 0, xplus), (before, 1, xminus),
        ))
    ]

    def query_multiply():
        for h in range(2):
            total = nt(lin[0, 0], wq[pl.ds(h * HALF, HALF), :]).astype(BF16)
            for o in range(8):
                ig[o % 2, o // 2, h] = total[64 * o : 64 * o + 64]

    def core_rows(which):
        return [
            lin[1, 0, pl.ds(pl.multiple_of(64 * (2 * n + which), 64), 64), :] for n in range(4)
        ]

    def key_multiply():
        left = jnp.concatenate(core_rows(core), axis=0)
        left = jnp.concatenate([left, swap_in[...]], axis=1)
        for n in range(4):
            pair_copies[n].wait_recv()
        for h in range(2):
            total = nt(left, wkv[pl.ds(h * HALF, HALF), :])
            for n in range(4):
                ig[core, n, h] = (
                    total[64 * n : 64 * n + 64] + ig[core, n, h].astype(F32)
                    + pair[n, h].astype(F32)
                ).astype(BF16)
            for n in ((0, 3), (1, 2))[h]:
                ring_x[n].start()

    def ring_second():
        for n, block in ((0, after), (1, before)):
            ring_x[n].wait_recv()
            ig[core, block, n] = (
                ig[core, block, n].astype(F32) + xring[n].astype(F32)
            ).astype(BF16)
            ring_x[4 + n].start()

    def ring_last():
        for n in (2, 3, 4, 5):
            ring_x[n].wait_recv()
        for h, first, second in ((0, 4, 3), (1, 2, 5)):
            ig_out[:, pl.ds(h * HALF, HALF)] = (
                ig[core, chip, h].astype(F32) + xring[first].astype(F32)
                + xring[second].astype(F32)
            ).astype(BF16)

    def store(n, src, dst):
        return pltpu.make_async_copy(src, dst, out_sem.at[n])

    store_ig = store(0, ig_out, ig_hbm)
    store_gq = store(1, gq_out, gq_hbm)
    store_gk = store(2, gk_out, gk_hbm)
    store_gv = store(3, gv_out, gv_hbm)
    store_go = store(4, go_out, go_hbm)

    for copy in ring_kv[:3] + (load_og, load_wo) + tuple(move_z):
        copy.start()
    for copy in (load_x, load_wk, load_wv) + tuple(move_w):
        copy.start()
    keys[latest, :] = k_ref[...]
    values[latest, :] = v_ref[...]
    lane = lax.broadcasted_iota(jnp.int32, (TILE, HD), 1)
    for n in range(ROWS // TILE):
        rows = slice(TILE * n, TILE * n + TILE)
        place = jnp.broadcast_to(place_ref[n : n + 1, :].astype(F32), (TILE, HD)).T
        angle = place * freq_ref[...]
        cos_ref[rows, :] = jnp.cos(angle)
        sine = jnp.sin(angle)
        sin_ref[rows, :] = jnp.where(lane < HD // 2, sine, -sine)
        row = lax.broadcasted_iota(jnp.int32, (TILE, HD), 0) + TILE * n
        reach = jnp.minimum(place.astype(jnp.int32), W - 1)
        low_ref[rows, :] = jnp.maximum(row - reach + 2 * ROWS, (2 - y) * ROWS)
    dkt[...] = jnp.zeros_like(dkt)
    dvt[...] = jnp.zeros_like(dvt)
    for n in range(2):
        ring_kv[n].wait_recv()
        ring_kv[3 + n].start()
    load_og.wait()
    load_wo.wait()
    dattn[...] = nn(og[...], wq[...]).astype(BF16)
    load_wq.start()
    for copy in move_z:
        copy.wait_recv()
    for copy in move_x[:2] + move_core[:1]:
        copy.start()
    for copy in ring_kv[2:]:
        copy.wait_recv()
    lax.fori_loop(0, ROWS // TILE, forward, 0)
    outer_multiply()
    outer_first((0, 1), (0, 1))
    outer_first((0,), (2, 3))
    lax.fori_loop(0, ROWS // TILE, backward, 0)
    gout[0] = dkt[:, oldest].astype(BF16)
    gout[1] = dvt[:, oldest].astype(BF16)
    gout[2] = dvt[:, middle].astype(BF16)
    for copy in ring_back[:3] + tuple(gather(0)[:2]):
        copy.start()
    load_wq.wait()
    query_multiply()
    for copy in pair_copies:
        copy.start()
    ring_back[0].wait_recv()
    gin[0] = (gin[0].astype(F32) + dkt[:, middle]).astype(BF16)
    ring_back[3].start()
    ring_back[1].wait_recv()
    ring_back[4].start()
    outer_first((1,), (2, 3))
    outer_second(0)
    for n in range(2):
        move_x[n].wait_recv()
        move_x[2 + n].start()
        move_core[1 + n].start()
    outer_second(1)
    for copy in ring_back[2:]:
        copy.wait_recv()
    key_grad = (dkt[:, latest] + gin[3].astype(F32)).T
    value_grad = (dvt[:, latest] + gin[2].astype(F32) + gin[4].astype(F32)).T
    lin[1, 0, :, :HD] = rotate(key_grad, cos_ref[...], sin_ref[...]).astype(BF16)
    lin[1, 0, :, HD:] = value_grad.astype(BF16)
    swap_out[...] = jnp.concatenate(core_rows(1 - core), axis=0)
    move_swap.start()
    for copy in gather(1)[:2]:
        copy.start()
    load_wk.wait()
    load_wv.wait()
    for copy in move_w:
        copy.wait_recv()
    move_swap.wait_recv()
    key_multiply()
    gather_relay(0)
    for copy in move_x[2:]:
        copy.wait_recv()
    move_core[3].start()
    outer_last(0)
    outer_last(1)
    load_x.wait()
    for copy in move_core + gather(0)[2:]:
        copy.wait_recv()
    inner_multiply(0)
    gather_relay(1)
    inner_second(0)
    inner_second(1)
    ring_second()
    inner_second(2)
    for copy in gather(1)[2:]:
        copy.wait_recv()
    inner_multiply(1)
    every = slice(0, 2 * HD)
    left, right = slice(0, HD), slice(HD, 2 * HD)
    inner_last(0, ((go_out, left, left),))
    inner_last(1, ((go_out, left, right),))
    store_go.start()
    inner_second(3)
    inner_last(2, ((gq_out, every, every),))
    store_gq.start()
    inner_last(3, ((gk_out, left, left), (gv_out, right, left)))
    store_gk.start()
    store_gv.start()
    ring_last()
    store_ig.start()
    for copy in (store_go, store_gq, store_gk, store_gv, store_ig):
        copy.wait()
    sent = list(ring_kv + ring_back) + move_z + move_x + move_core + move_w + [move_swap]
    sent += pair_copies + ring_x
    for s in range(4):
        sent += inner(s)
    for n in range(2):
        sent += gather(n) + outer(n)
    for copy in sent:
        copy.wait_send()


OUTS = (
    jax.ShapeDtypeStruct((64, D), BF16),
    jax.ShapeDtypeStruct((OWN, 2 * HD), F32),
    jax.ShapeDtypeStruct((OWN, HD), F32),
    jax.ShapeDtypeStruct((OWN, HD), F32),
    jax.ShapeDtypeStruct((OWN, 2 * HD), F32),
)


def fused(*operands):
    vmem = pl.BlockSpec(memory_space=pltpu.VMEM)
    anywhere = pl.BlockSpec(memory_space=pl.ANY)
    dma = pltpu.SemaphoreType.DMA
    buffers = (
        ((ROWS, HD), jnp.int32),
        ((ROWS, HD), F32),
        ((ROWS, HD), F32),
        ((BAND, HD), BF16),
        ((BAND, HD), BF16),
        ((ROWS, HD), BF16),
        ((ROWS, D), BF16),
        ((4, ROWS, SPAN), BF16),
        ((D, 2 * HD), BF16),
        ((D, 4 * HD), BF16),
        ((ROWS, 2 * HD), BF16),
        ((ROWS, 2 * HD), BF16),
        ((2, 4, ROWS, 2 * HD), BF16),
        ((ROWS // 2, 2 * HD), BF16),
        ((ROWS // 2, 2 * HD), BF16),
        ((ROWS // TILE, 2 * TILE, WINDOW), F32),
        ((HD, BAND), F32),
        ((HD, BAND), F32),
        ((3, HD, ROWS), BF16),
        ((5, HD, ROWS), BF16),
        ((SPAN, 2 * HD), F32),
        ((2, 16, OWN, HD), BF16),
        ((2, 6, 2, OWN, HD), BF16),
        ((2, 4, OWN, HD), BF16),
        ((2, 4, OWN, 2 * HD), BF16),
        ((2, 6, TOP, HD), BF16),
        ((2, 6, TOP, 2 * HD), BF16),
        ((2, 4, 2, 64, HALF), BF16),
        ((4, 2, 64, HALF), BF16),
        ((6, 64, HALF), BF16),
    )
    counts = ((5,), (5,), (2, 6), (4, 6), (4,), (6,), (14,), (2, 4))
    return pl.pallas_call(
        fused_kernel,
        out_shape=OUTS,
        in_specs=[vmem] * 5 + [anywhere] * 6,
        out_specs=(anywhere,) * 5,
        scratch_shapes=[pltpu.VMEM(out.shape, out.dtype) for out in OUTS]
        + [pltpu.VMEM(*buffer) for buffer in buffers]
        + [dma((8,)), dma((5,))]
        + [dma(count) for count in counts for _ in range(2)],
        compiler_params=pltpu.CompilerParams(
            collective_id=0, has_side_effects=True, vmem_limit_bytes=66_900_000
        ),
        name="fused",
    )(*operands)


def finish_kernel(*refs):
    sources, targets, buffers, sems = refs[:5], refs[5:10], refs[10:15], refs[15]
    order = (0, 1, 4, 2, 3)
    loads = [pltpu.make_async_copy(sources[n], buffers[n], sems.at[0, n]) for n in range(5)]
    stores = [pltpu.make_async_copy(buffers[n], targets[n], sems.at[1, n]) for n in range(5)]
    for n in order:
        loads[n].start()
    for n in order:
        loads[n].wait()
        stores[n].start()
    for n in order:
        stores[n].wait()


def finish(*results):
    anywhere = pl.BlockSpec(memory_space=pl.ANY)
    return pl.pallas_call(
        finish_kernel, out_shape=OUTS, in_specs=[anywhere] * 5, out_specs=(anywhere,) * 5,
        scratch_shapes=[pltpu.VMEM(out.shape, out.dtype) for out in OUTS]
        + [pltpu.SemaphoreType.DMA((2, 5))],
        compiler_params=pltpu.CompilerParams(vmem_limit_bytes=66_900_000),
        name="finish",
    )(*results)


def on_device(
    inputs, queries, key_states, value_states, out_grad, positions,
    w_query, w_key, w_value, w_output,
):
    index = np.arange(HD) % (HD // 2)
    freq = jnp.asarray((10000.0 ** (index * (-2.0 / HD))).astype(np.float32)[None, :])
    return finish(
        *fused(
            queries, key_states, value_states, positions.reshape(ROWS // TILE, TILE), freq,
            inputs, out_grad, w_query, w_key, w_value, w_output,
        )
    )


def solution(mesh):
    rows = ("dp", "context")
    return jax.shard_map(
        on_device,
        mesh=mesh,
        in_specs=(
            P(rows, None), P(rows, "tensor"), P(rows, "tensor"), P(rows, "tensor"),
            P(rows, None), P(rows), P(None, "tensor"), P(None, "tensor"),
            P(None, "tensor"), P(None, "tensor"),
        ),
        out_specs=(
            P(("dp", "context", "tensor"), None), P(rows, "tensor"), P(rows, "tensor"),
            P(rows, "tensor"), P(rows, "tensor"),
        ),
        check_vma=False,
    )
```

time: 93.6 us -> 74 us (0.79)
  Pallas kernels: 84.1 us -> 73.2 us
  local copies, waits for them, and re-layouts: 5.74 us -> 0 us
  other arithmetic: 2.77 us -> 0 us
    pallas_call x2, Pallas kernels: 84.1 us -> 73.2 us  [the longest x1 70.8 us: fused(): pl.pallas_call(fused_kernel, out_shape=OUTS, in_specs=[vmem] * 5 + [anywh...]
    unnamed x10 -> x0, local copies, waits for them, and re-layouts: 4.88 us -> none
    concatenate x1 -> x0, other arithmetic: 1 us -> none  [on_device(): cosine = jnp.concatenate([cosine, cosine], axis=1)]
    sin x1 -> x0, other arithmetic: 0.99 us -> none  [on_device(): cosine, sine = (jnp.cos(angle), jnp.sin(angle))]
where the time goes in v3:
time: 74 us; the launch traced here: 73.8 us
  Pallas kernels  73.2 us (99%)
    pallas_call x1, Pallas kernels, fused(): pl.pallas_call(fused_kernel, out_shape=OUTS, in_specs=[vmem] * 5 + [anywh...  70.8 us
    pallas_call x1, Pallas kernels, finish(): pl.pallas_call(finish_kernel, out_shape=OUTS, in_specs=[anywhere] * 5, ou...  2.37 us

profile of v3, /device:TPU:0, one launch (start us, length us, event | category | flops | bytes accessed | tf_op | source)
XLA Modules:
  0.0 73.8 jit_solution(4596761207801691951)
XLA Ops:
  0.6 70.8 %fused.1 = (bf16[64,5376]{1,0:T(8,128)(2,1)}, f32[336,256]{1,0:T(8,128)}, f32[336,128]{1,0:T(8,128)}, f32[336,128]{1,0:T(8,128)}, f32[336,256]{1,0:T(8,128)}) custom-call(bf16[512,256]{1,0:T(8,128)(2,1)} %q_ref.1, bf16[512,128]{1,0:T(8,128)(2,1)} %k_ref.1, bf16[512,128]{1,0:T(8,128)(2,1)} %v_ref.1, s32[4,128]{1,0:T(4,128)} %bitcast.1, ...), custom_call_target="tpu_custom_call" | custom-call | tf_op jit(solution)/shard_map/fused/pallas_call | solution.py:566
  71.5 2.4 %finish.1 = (bf16[64,5376]{1,0:T(8,128)(2,1)}, f32[336,256]{1,0:T(8,128)}, f32[336,128]{1,0:T(8,128)}, f32[336,128]{1,0:T(8,128)}, f32[336,256]{1,0:T(8,128)}) custom-call(bf16[64,5376]{1,0:T(8,128)(2,1)} %get-tuple-element.10.refs_0_, f32[336,256]{1,0:T(8,128)} %get-tuple-element.11.refs_1_, f32[336,128]{1,0:T(8,128)} %get-tuple-element.12.refs_2_, ...), custom_call_target="tpu_custom_call" | custom-call | tf_op jit(solution)/shard_map/finish/pallas_call | solution.py:598

commit v4 on v3

--- a/solution.py
+++ b/solution.py
@@ -20,6 +20,7 @@
 HALF = D // 2
 SPAN = 1408
 TOP = 176
+LOG2E = 1.4426950408889634
 F32 = jnp.float32
 BF16 = jnp.bfloat16
 MESH = pl.DeviceIdType.MESH
@@ -43,11 +44,11 @@
 
 
 def fused_kernel(
-    q_ref, k_ref, v_ref, place_ref, freq_ref,
+    q_hbm, k_hbm, v_hbm, place_hbm, freq_hbm,
     x_hbm, og_hbm, wq_hbm, wk_hbm, wv_hbm, wo_hbm,
     ig_hbm, gq_hbm, gk_hbm, gv_hbm, go_hbm,
     ig_out, gq_out, gk_out, gv_out, go_out, low_ref, cos_ref, sin_ref,
-    keys, values, relay, og, wide_x, wq, wkv, dattn, attn, lin, swap_out, swap_in,
+    q_ref, place_ref, freq_ref, keys, values, relay, og, wide_x, wq, wkv, dattn, attn, lin, swap_out, swap_in,
     probs, dkt, dvt, gout, gin, product,
     parts, near, mid_half, mid_full, far_half, far_full, ig, pair, xring, load_sem, out_sem,
     a_send, a_recv, b_send, b_recv, c_send, c_recv, e_send, e_recv,
@@ -79,9 +80,18 @@
     load_wq = load(5, wq_hbm, wq)
     load_wk = load(6, wk_hbm, wkv.at[:, pl.ds(0, HD)])
     load_wv = load(7, wv_hbm, wkv.at[:, pl.ds(HD, HD)])
+    small = [
+        load(8 + n, src, dst)
+        for n, (src, dst) in enumerate((
+            (place_hbm, place_ref), (freq_hbm, freq_ref), (q_hbm, q_ref),
+            (k_hbm, keys.at[latest]), (v_hbm, values.at[latest]),
+        ))
+    ]
     barrier = pltpu.get_barrier_semaphore()
-    for device in (yplus, yminus, zplus, zminus, zfar, xplus, xminus, partner):
+    for device in (zfar, yplus, yminus, zplus, zminus, xplus, xminus, partner):
         pl.semaphore_signal(barrier, inc=1, device_id=device, device_id_type=MESH)
+    for copy in small:
+        copy.start()
     pl.semaphore_wait(barrier, 8)
 
     lines = (("dp", z, "context", y), ("context", y, "dp", z))
@@ -96,9 +106,9 @@
         return remote(src, dst, a_send.at[n], a_recv.at[n], device)
 
     ring_kv = (
-        ring(0, k_ref, keys.at[middle], yplus),
-        ring(1, v_ref, relay, yminus),
-        ring(2, v_ref, values.at[middle], yplus),
+        ring(0, k_hbm, keys.at[middle], yplus),
+        ring(1, v_hbm, relay, yminus),
+        ring(2, v_hbm, values.at[middle], yplus),
         ring(3, keys.at[middle], keys.at[oldest], yplus),
         ring(4, relay, values.at[oldest], yminus),
     )
@@ -215,11 +225,13 @@
         low = jnp.concatenate([low, low], axis=0)
         row = lax.broadcasted_iota(jnp.int32, (2 * TILE, 1), 0) % TILE
         col = lax.broadcasted_iota(jnp.int32, (2 * TILE, WINDOW), 1)
-        allowed = (col >= low) & (col <= row + W)
-        scores = jnp.where(allowed, nt(stacked(q_ref, rows), keys[wide, :]) * scale, -1e30)
+        scores = nt(stacked(q_ref, rows), keys[wide, :])
+        before = jnp.where(col[:, :W] >= low, scores[:, :W], -1e30)
+        edge = (col[:, W:] >= low) & (col[:, W:] <= row + W)
+        scores = jnp.concatenate([before, jnp.where(edge, scores[:, W:], -1e30)], axis=1)
         top = jnp.max(scores, axis=-1, keepdims=True)
-        raised = jnp.exp(scores - top)
-        prob = raised / jnp.sum(raised, axis=-1, keepdims=True)
+        raised = jnp.exp2((scores - top) * (scale * LOG2E))
+        prob = raised * (1.0 / jnp.sum(raised, axis=-1, keepdims=True))
         probs[i] = prob
         result = nn(prob.astype(BF16), values[wide, :]).astype(BF16)
         attn[rows, :HD] = result[:TILE]
@@ -296,16 +308,14 @@
             ).astype(BF16)
         inner_start(kind)
 
-    def inner_multiply(r):
-        product[...] = jnp.zeros_like(product)
-
-        def body(j, carry):
-            product[...] += lax.dot_general(
+    def inner_multiply(r, *blocks):
+        for j in blocks:
+            term = lax.dot_general(
                 wide_x[j], lin[r, j], (((0,), (0,)), ((), ())), preferred_element_type=F32
             )
-            return carry
-
-        lax.fori_loop(0, 4, body, 0)
+            product[...] = term if j == 0 else product[...] + term
+
+    def inner_round(r):
         for block in range(4):
             start = pl.multiple_of(64 * lax.rem(z, 2) + OWN * block, 16)
             mid_full[r, block] = product[pl.ds(start, OWN), :].astype(BF16)
@@ -371,8 +381,7 @@
                     total[64 * n : 64 * n + 64] + ig[core, n, h].astype(F32)
                     + pair[n, h].astype(F32)
                 ).astype(BF16)
-            for n in ((0, 3), (1, 2))[h]:
-                ring_x[n].start()
+            ring_x[h].start()
 
     def ring_second():
         for n, block in ((0, after), (1, before)):
@@ -400,12 +409,12 @@
     store_gv = store(3, gv_out, gv_hbm)
     store_go = store(4, go_out, go_hbm)
 
-    for copy in ring_kv[:3] + (load_og, load_wo) + tuple(move_z):
+    for copy in ring_kv[:2] + (load_og, load_wo) + tuple(move_z):
         copy.start()
     for copy in (load_x, load_wk, load_wv) + tuple(move_w):
         copy.start()
-    keys[latest, :] = k_ref[...]
-    values[latest, :] = v_ref[...]
+    for copy in small[:2]:
+        copy.wait()
     lane = lax.broadcasted_iota(jnp.int32, (TILE, HD), 1)
     for n in range(ROWS // TILE):
         rows = slice(TILE * n, TILE * n + TILE)
@@ -419,6 +428,8 @@
         low_ref[rows, :] = jnp.maximum(row - reach + 2 * ROWS, (2 - y) * ROWS)
     dkt[...] = jnp.zeros_like(dkt)
     dvt[...] = jnp.zeros_like(dvt)
+    ring_kv[0].wait_send()
+    ring_kv[2].start()
     for n in range(2):
         ring_kv[n].wait_recv()
         ring_kv[3 + n].start()
@@ -430,34 +441,38 @@
         copy.wait_recv()
     for copy in move_x[:2] + move_core[:1]:
         copy.start()
+    for copy in small[2:]:
+        copy.wait()
     for copy in ring_kv[2:]:
         copy.wait_recv()
     lax.fori_loop(0, ROWS // TILE, forward, 0)
-    outer_multiply()
-    outer_first((0, 1), (0, 1))
-    outer_first((0,), (2, 3))
     lax.fori_loop(0, ROWS // TILE, backward, 0)
     gout[0] = dkt[:, oldest].astype(BF16)
     gout[1] = dvt[:, oldest].astype(BF16)
     gout[2] = dvt[:, middle].astype(BF16)
-    for copy in ring_back[:3] + tuple(gather(0)[:2]):
+    for copy in ring_back[:2] + tuple(gather(0)[:2]):
         copy.start()
+    outer_multiply()
+    outer_first((1,), (0,))
+    ring_back[0].wait_send()
+    ring_back[2].start()
     load_wq.wait()
     query_multiply()
     for copy in pair_copies:
         copy.start()
+    outer_first((0,), (0, 1))
     ring_back[0].wait_recv()
     gin[0] = (gin[0].astype(F32) + dkt[:, middle]).astype(BF16)
     ring_back[3].start()
     ring_back[1].wait_recv()
     ring_back[4].start()
-    outer_first((1,), (2, 3))
-    outer_second(0)
+    load_x.wait()
+    inner_multiply(0, 0)
+    gather_relay(0)
     for n in range(2):
         move_x[n].wait_recv()
         move_x[2 + n].start()
         move_core[1 + n].start()
-    outer_second(1)
     for copy in ring_back[2:]:
         copy.wait_recv()
     key_grad = (dkt[:, latest] + gin[3].astype(F32)).T
@@ -468,47 +483,55 @@
     move_swap.start()
     for copy in gather(1)[:2]:
         copy.start()
+    outer_first((1,), (1, 2, 3))
     load_wk.wait()
     load_wv.wait()
     for copy in move_w:
         copy.wait_recv()
     move_swap.wait_recv()
     key_multiply()
-    gather_relay(0)
     for copy in move_x[2:]:
         copy.wait_recv()
     move_core[3].start()
-    outer_last(0)
-    outer_last(1)
-    load_x.wait()
+    outer_first((0,), (2, 3))
     for copy in move_core + gather(0)[2:]:
         copy.wait_recv()
-    inner_multiply(0)
+    inner_multiply(0, 3, 1, 2)
+    inner_round(0)
     gather_relay(1)
-    inner_second(0)
-    inner_second(1)
+    outer_second(1)
+    inner_multiply(1, 0, 3, 1)
+    for n in range(2):
+        ring_x[n].wait_send()
+        ring_x[2 + n].start()
     ring_second()
+    outer_second(0)
     inner_second(2)
     for copy in gather(1)[2:]:
         copy.wait_recv()
-    inner_multiply(1)
+    inner_multiply(1, 2)
+    inner_round(1)
+    outer_last(1)
+    outer_last(0)
+    inner_second(3)
+    inner_second(1)
+    inner_second(0)
     every = slice(0, 2 * HD)
     left, right = slice(0, HD), slice(HD, 2 * HD)
-    inner_last(0, ((go_out, left, left),))
-    inner_last(1, ((go_out, left, right),))
-    store_go.start()
-    inner_second(3)
     inner_last(2, ((gq_out, every, every),))
     store_gq.start()
     inner_last(3, ((gk_out, left, left), (gv_out, right, left)))
     store_gk.start()
     store_gv.start()
+    inner_last(1, ((go_out, left, right),))
+    inner_last(0, ((go_out, left, left),))
+    store_go.start()
     ring_last()
     store_ig.start()
     for copy in (store_go, store_gq, store_gk, store_gv, store_ig):
         copy.wait()
-    sent = list(ring_kv + ring_back) + move_z + move_x + move_core + move_w + [move_swap]
-    sent += pair_copies + ring_x
+    sent = list(ring_kv[1:] + ring_back[1:]) + move_z + move_x + move_core + move_w + [move_swap]
+    sent += pair_copies + ring_x[2:]
     for s in range(4):
         sent += inner(s)
     for n in range(2):
@@ -527,13 +550,15 @@
 
 
 def fused(*operands):
-    vmem = pl.BlockSpec(memory_space=pltpu.VMEM)
     anywhere = pl.BlockSpec(memory_space=pl.ANY)
     dma = pltpu.SemaphoreType.DMA
     buffers = (
         ((ROWS, HD), jnp.int32),
         ((ROWS, HD), F32),
         ((ROWS, HD), F32),
+        ((ROWS, 2 * HD), BF16),
+        ((ROWS // TILE, TILE), jnp.int32),
+        ((1, HD), F32),
         ((BAND, HD), BF16),
         ((BAND, HD), BF16),
         ((ROWS, HD), BF16),
@@ -566,11 +591,11 @@
     return pl.pallas_call(
         fused_kernel,
         out_shape=OUTS,
-        in_specs=[vmem] * 5 + [anywhere] * 6,
+        in_specs=[anywhere] * 11,
         out_specs=(anywhere,) * 5,
         scratch_shapes=[pltpu.VMEM(out.shape, out.dtype) for out in OUTS]
         + [pltpu.VMEM(*buffer) for buffer in buffers]
-        + [dma((8,)), dma((5,))]
+        + [dma((13,)), dma((5,))]
         + [dma(count) for count in counts for _ in range(2)],
         compiler_params=pltpu.CompilerParams(
             collective_id=0, has_side_effects=True, vmem_limit_bytes=66_900_000

time: 74 us -> 69.6 us (0.941); the launches traced: 73.8 us -> 68.4 us
  Pallas kernels: 73.2 us -> 67.6 us
    pallas_call x1, Pallas kernels: 70.8 us -> 65.2 us  [fused(): pl.pallas_call(fused_kernel, out_shape=OUTS, in_specs=[anywhere] * 11, ou...]
where the time goes in v4:
time: 69.6 us; the launch traced here: 68.4 us
  Pallas kernels  67.6 us (97%)
  between operations  0.8 us (1%)
    pallas_call x1, Pallas kernels, fused(): pl.pallas_call(fused_kernel, out_shape=OUTS, in_specs=[anywhere] * 11, ou...  65.2 us
    pallas_call x1, Pallas kernels, finish(): pl.pallas_call(finish_kernel, out_shape=OUTS, in_specs=[anywhere] * 5, ou...  2.37 us

profile of v4, /device:TPU:0, one launch (start us, length us, event | category | flops | bytes accessed | tf_op | source)
XLA Modules:
  0.0 68.4 jit_solution(17247702924792818247)
XLA Ops:
  0.6 65.2 %fused.1 = (bf16[64,5376]{1,0:T(8,128)(2,1)}, f32[336,256]{1,0:T(8,128)}, f32[336,128]{1,0:T(8,128)}, f32[336,128]{1,0:T(8,128)}, f32[336,256]{1,0:T(8,128)}) custom-call(bf16[512,256]{1,0:T(8,128)(2,1)} %q_hbm.1, bf16[512,128]{1,0:T(8,128)(2,1)} %k_hbm.1, bf16[512,128]{1,0:T(8,128)(2,1)} %v_hbm.1, s32[4,128]{1,0:T(4,128)} %bitcast.1, ...), custom_call_target="tpu_custom_call" | custom-call | tf_op jit(solution)/shard_map/fused/pallas_call | solution.py:591
  65.8 2.4 %finish.1 = (bf16[64,5376]{1,0:T(8,128)(2,1)}, f32[336,256]{1,0:T(8,128)}, f32[336,128]{1,0:T(8,128)}, f32[336,128]{1,0:T(8,128)}, f32[336,256]{1,0:T(8,128)}) custom-call(bf16[64,5376]{1,0:T(8,128)(2,1)} %get-tuple-element.10.refs_0_, f32[336,256]{1,0:T(8,128)} %get-tuple-element.11.refs_1_, f32[336,128]{1,0:T(8,128)} %get-tuple-element.12.refs_2_, ...), custom_call_target="tpu_custom_call" | custom-call | tf_op jit(solution)/shard_map/finish/pallas_call | solution.py:623

commit v5 on v4

--- a/solution.py
+++ b/solution.py
@@ -233,7 +233,9 @@
         raised = jnp.exp2((scores - top) * (scale * LOG2E))
         prob = raised * (1.0 / jnp.sum(raised, axis=-1, keepdims=True))
         probs[i] = prob
-        result = nn(prob.astype(BF16), values[wide, :]).astype(BF16)
+        half = prob.astype(BF16)
+        result = nn(half, values[wide, :]).astype(BF16)
+        dvt[:, wide] += nn(stacked(dattn, rows).T, half)
         attn[rows, :HD] = result[:TILE]
         attn[rows, HD:] = result[TILE:]
         return carry
@@ -255,7 +257,6 @@
             dq[TILE:], cos_ref[rows, :], sin_ref[rows, :]
         ).astype(BF16)
         dkt[:, wide] += nn(stacked(q_ref, rows).T, dscores)
-        dvt[:, wide] += nn(grad.T, prob.astype(BF16))
         return carry
 
     def outer_multiply():
@@ -437,25 +438,27 @@
     load_wo.wait()
     dattn[...] = nn(og[...], wq[...]).astype(BF16)
     load_wq.start()
-    for copy in move_z:
-        copy.wait_recv()
-    for copy in move_x[:2] + move_core[:1]:
-        copy.start()
     for copy in small[2:]:
         copy.wait()
     for copy in ring_kv[2:]:
         copy.wait_recv()
-    lax.fori_loop(0, ROWS // TILE, forward, 0)
-    lax.fori_loop(0, ROWS // TILE, backward, 0)
-    gout[0] = dkt[:, oldest].astype(BF16)
+    lax.fori_loop(0, 2, forward, 0, unroll=True)
+    for copy in move_z:
+        copy.wait_recv()
+    for copy in move_x[:2] + move_core[:1]:
+        copy.start()
+    lax.fori_loop(2, ROWS // TILE, forward, 0, unroll=True)
     gout[1] = dvt[:, oldest].astype(BF16)
     gout[2] = dvt[:, middle].astype(BF16)
-    for copy in ring_back[:2] + tuple(gather(0)[:2]):
+    for copy in ring_back[1:3]:
+        copy.start()
+    lax.fori_loop(0, ROWS // TILE, backward, 0, unroll=True)
+    gout[0] = dkt[:, oldest].astype(BF16)
+    for copy in ring_back[:1] + tuple(gather(0)[:2]):
         copy.start()
     outer_multiply()
-    outer_first((1,), (0,))
-    ring_back[0].wait_send()
-    ring_back[2].start()
+    ring_back[1].wait_recv()
+    ring_back[4].start()
     load_wq.wait()
     query_multiply()
     for copy in pair_copies:
@@ -464,15 +467,13 @@
     ring_back[0].wait_recv()
     gin[0] = (gin[0].astype(F32) + dkt[:, middle]).astype(BF16)
     ring_back[3].start()
-    ring_back[1].wait_recv()
-    ring_back[4].start()
     load_x.wait()
     inner_multiply(0, 0)
-    gather_relay(0)
     for n in range(2):
         move_x[n].wait_recv()
         move_x[2 + n].start()
-        move_core[1 + n].start()
+    outer_first((1,), (0,))
+    gather_relay(0)
     for copy in ring_back[2:]:
         copy.wait_recv()
     key_grad = (dkt[:, latest] + gin[3].astype(F32)).T
@@ -481,14 +482,16 @@
     lin[1, 0, :, HD:] = value_grad.astype(BF16)
     swap_out[...] = jnp.concatenate(core_rows(1 - core), axis=0)
     move_swap.start()
+    for copy in move_core[1:3]:
+        copy.start()
     for copy in gather(1)[:2]:
         copy.start()
-    outer_first((1,), (1, 2, 3))
     load_wk.wait()
     load_wv.wait()
     for copy in move_w:
         copy.wait_recv()
     move_swap.wait_recv()
+    outer_first((1,), (1, 2, 3))
     key_multiply()
     for copy in move_x[2:]:
         copy.wait_recv()
@@ -498,13 +501,13 @@
         copy.wait_recv()
     inner_multiply(0, 3, 1, 2)
     inner_round(0)
-    gather_relay(1)
-    outer_second(1)
-    inner_multiply(1, 0, 3, 1)
     for n in range(2):
         ring_x[n].wait_send()
         ring_x[2 + n].start()
+    gather_relay(1)
     ring_second()
+    outer_second(1)
+    inner_multiply(1, 0, 3, 1)
     outer_second(0)
     inner_second(2)
     for copy in gather(1)[2:]:
@@ -530,7 +533,7 @@
     store_ig.start()
     for copy in (store_go, store_gq, store_gk, store_gv, store_ig):
         copy.wait()
-    sent = list(ring_kv[1:] + ring_back[1:]) + move_z + move_x + move_core + move_w + [move_swap]
+    sent = list(ring_kv[1:] + ring_back) + move_z + move_x + move_core + move_w + [move_swap]
     sent += pair_copies + ring_x[2:]
     for s in range(4):
         sent += inner(s)

time: 69.6 us -> 68.1 us (0.978); the launches traced: 68.4 us -> 68 us
  no operation moved by 1% of the time
where the time goes in v5:
time: 68.1 us; the launch traced here: 68 us
  Pallas kernels  67.1 us (99%)
  between operations  0.8 us (1%)
    pallas_call x1, Pallas kernels, fused(): pl.pallas_call(fused_kernel, out_shape=OUTS, in_specs=[anywhere] * 11, ou...  64.8 us
    pallas_call x1, Pallas kernels, finish(): pl.pallas_call(finish_kernel, out_shape=OUTS, in_specs=[anywhere] * 5, ou...  2.37 us

profile of v5, /device:TPU:0, one launch (start us, length us, event | category | flops | bytes accessed | tf_op | source)
XLA Modules:
  0.0 68.0 jit_solution(17172380849436841994)
XLA Ops:
  0.6 64.8 %fused.1 = (bf16[64,5376]{1,0:T(8,128)(2,1)}, f32[336,256]{1,0:T(8,128)}, f32[336,128]{1,0:T(8,128)}, f32[336,128]{1,0:T(8,128)}, f32[336,256]{1,0:T(8,128)}) custom-call(bf16[512,256]{1,0:T(8,128)(2,1)} %q_hbm.1, bf16[512,128]{1,0:T(8,128)(2,1)} %k_hbm.1, bf16[512,128]{1,0:T(8,128)(2,1)} %v_hbm.1, s32[4,128]{1,0:T(4,128)} %bitcast.1, ...), custom_call_target="tpu_custom_call" | custom-call | tf_op jit(solution)/shard_map/fused/pallas_call | solution.py:594
  65.4 2.4 %finish.1 = (bf16[64,5376]{1,0:T(8,128)(2,1)}, f32[336,256]{1,0:T(8,128)}, f32[336,128]{1,0:T(8,128)}, f32[336,128]{1,0:T(8,128)}, f32[336,256]{1,0:T(8,128)}) custom-call(bf16[64,5376]{1,0:T(8,128)(2,1)} %get-tuple-element.10.refs_0_, f32[336,256]{1,0:T(8,128)} %get-tuple-element.11.refs_1_, f32[336,128]{1,0:T(8,128)} %get-tuple-element.12.refs_2_, ...), custom_call_target="tpu_custom_call" | custom-call | tf_op jit(solution)/shard_map/finish/pallas_call | solution.py:626

commit v6 on v5

--- a/solution.py
+++ b/solution.py
@@ -46,11 +46,10 @@
 def fused_kernel(
     q_hbm, k_hbm, v_hbm, place_hbm, freq_hbm,
     x_hbm, og_hbm, wq_hbm, wk_hbm, wv_hbm, wo_hbm,
-    ig_hbm, gq_hbm, gk_hbm, gv_hbm, go_hbm,
     ig_out, gq_out, gk_out, gv_out, go_out, low_ref, cos_ref, sin_ref,
     q_ref, place_ref, freq_ref, keys, values, relay, og, wide_x, wq, wkv, dattn, attn, lin, swap_out, swap_in,
     probs, dkt, dvt, gout, gin, product,
-    parts, near, mid_half, mid_full, far_half, far_full, ig, pair, xring, load_sem, out_sem,
+    parts, near, mid_half, mid_full, far_half, far_full, ig, pair, xring, load_sem,
     a_send, a_recv, b_send, b_recv, c_send, c_recv, e_send, e_recv,
     f_send, f_recv, g_send, g_recv, h_send, h_recv, l_send, l_recv,
 ):
@@ -400,15 +399,6 @@
                 ig[core, chip, h].astype(F32) + xring[first].astype(F32)
                 + xring[second].astype(F32)
             ).astype(BF16)
-
-    def store(n, src, dst):
-        return pltpu.make_async_copy(src, dst, out_sem.at[n])
-
-    store_ig = store(0, ig_out, ig_hbm)
-    store_gq = store(1, gq_out, gq_hbm)
-    store_gk = store(2, gk_out, gk_hbm)
-    store_gv = store(3, gv_out, gv_hbm)
-    store_go = store(4, go_out, go_hbm)
 
     for copy in ring_kv[:2] + (load_og, load_wo) + tuple(move_z):
         copy.start()
@@ -522,17 +512,10 @@
     every = slice(0, 2 * HD)
     left, right = slice(0, HD), slice(HD, 2 * HD)
     inner_last(2, ((gq_out, every, every),))
-    store_gq.start()
     inner_last(3, ((gk_out, left, left), (gv_out, right, left)))
-    store_gk.start()
-    store_gv.start()
     inner_last(1, ((go_out, left, right),))
     inner_last(0, ((go_out, left, left),))
-    store_go.start()
     ring_last()
-    store_ig.start()
-    for copy in (store_go, store_gq, store_gk, store_gv, store_ig):
-        copy.wait()
     sent = list(ring_kv[1:] + ring_back) + move_z + move_x + move_core + move_w + [move_swap]
     sent += pair_copies + ring_x[2:]
     for s in range(4):
@@ -593,43 +576,37 @@
     counts = ((5,), (5,), (2, 6), (4, 6), (4,), (6,), (14,), (2, 4))
     return pl.pallas_call(
         fused_kernel,
-        out_shape=OUTS,
+        out_shape=tuple(pltpu.VMEM(out.shape, out.dtype) for out in OUTS),
         in_specs=[anywhere] * 11,
-        out_specs=(anywhere,) * 5,
-        scratch_shapes=[pltpu.VMEM(out.shape, out.dtype) for out in OUTS]
-        + [pltpu.VMEM(*buffer) for buffer in buffers]
-        + [dma((13,)), dma((5,))]
+        out_specs=(pl.BlockSpec(memory_space=pltpu.VMEM),) * 5,
+        scratch_shapes=[pltpu.VMEM(*buffer) for buffer in buffers]
+        + [dma((13,))]
         + [dma(count) for count in counts for _ in range(2)],
         compiler_params=pltpu.CompilerParams(
-            collective_id=0, has_side_effects=True, vmem_limit_bytes=66_900_000
+            collective_id=0, has_side_effects=True, vmem_limit_bytes=61_000_000
         ),
         name="fused",
     )(*operands)
 
 
 def finish_kernel(*refs):
-    sources, targets, buffers, sems = refs[:5], refs[5:10], refs[10:15], refs[15]
-    order = (0, 1, 4, 2, 3)
-    loads = [pltpu.make_async_copy(sources[n], buffers[n], sems.at[0, n]) for n in range(5)]
-    stores = [pltpu.make_async_copy(buffers[n], targets[n], sems.at[1, n]) for n in range(5)]
-    for n in order:
-        loads[n].start()
-    for n in order:
-        loads[n].wait()
-        stores[n].start()
-    for n in order:
-        stores[n].wait()
+    sources, targets, sems = refs[:5], refs[5:10], refs[10]
+    stores = [pltpu.make_async_copy(sources[n], targets[n], sems.at[n]) for n in range(5)]
+    for store in stores:
+        store.start()
+    for store in stores:
+        store.wait()
 
 
 def finish(*results):
     anywhere = pl.BlockSpec(memory_space=pl.ANY)
     return pl.pallas_call(
-        finish_kernel, out_shape=OUTS, in_specs=[anywhere] * 5, out_specs=(anywhere,) * 5,
-        scratch_shapes=[pltpu.VMEM(out.shape, out.dtype) for out in OUTS]
-        + [pltpu.SemaphoreType.DMA((2, 5))],
-        compiler_params=pltpu.CompilerParams(vmem_limit_bytes=66_900_000),
+        finish_kernel, out_shape=OUTS,
+        in_specs=[pl.BlockSpec(memory_space=pltpu.VMEM)] * 5, out_specs=(anywhere,) * 5,
+        scratch_shapes=[pltpu.SemaphoreType.DMA((5,))],
+        compiler_params=pltpu.CompilerParams(vmem_limit_bytes=8 << 20),
         name="finish",
-    )(*results)
+    )(*(pltpu.with_memory_space_constraint(result, pltpu.VMEM) for result in results))
 
 
 def on_device(

time: 68.1 us -> 66 us (0.969)
  Pallas kernels: 67.1 us -> 65.1 us
    pallas_call x2, Pallas kernels: 67.1 us -> 65.1 us  [the longest x1 63.9 us: fused(): pl.pallas_call(fused_kernel, out_shape=tuple((pltpu.VMEM(out.shape, out.d...]
where the time goes in v6:
time: 66 us; the launch traced here: 65.9 us
  Pallas kernels  65.1 us (99%)
  between operations  0.8 us (1%)
    pallas_call x1, Pallas kernels, fused(): pl.pallas_call(fused_kernel, out_shape=tuple((pltpu.VMEM(out.shape, out.d...  63.9 us

profile of v6, /device:TPU:0, one launch (start us, length us, event | category | flops | bytes accessed | tf_op | source)
XLA Modules:
  0.0 65.9 jit_solution(6307798064249836261)
XLA Ops:
  0.6 63.9 %fused.1 = (bf16[64,5376]{1,0:T(8,128)(2,1)S(1)}, f32[336,256]{1,0:T(8,128)S(1)}, f32[336,128]{1,0:T(8,128)S(1)}, f32[336,128]{1,0:T(8,128)S(1)}, f32[336,256]{1,0:T(8,128)S(1)}) custom-call(bf16[512,256]{1,0:T(8,128)(2,1)} %q_hbm.1, bf16[512,128]{1,0:T(8,128)(2,1)} %k_hbm.1, bf16[512,128]{1,0:T(8,128)(2,1)} %v_hbm.1, s32[4,128]{1,0:T(4,128)} %bitcast.1, ...), custom_call_target="tpu_custom_call" | custom-call | tf_op jit(solution)/shard_map/fused/pallas_call | solution.py:577
  64.5 1.2 %finish.1 = (bf16[64,5376]{1,0:T(8,128)(2,1)}, f32[336,256]{1,0:T(8,128)}, f32[336,128]{1,0:T(8,128)}, f32[336,128]{1,0:T(8,128)}, f32[336,256]{1,0:T(8,128)}) custom-call(bf16[64,5376]{1,0:T(8,128)(2,1)S(1)} %get-tuple-element.10.refs_0_, f32[336,256]{1,0:T(8,128)S(1)} %get-tuple-element.11.refs_1_, f32[336,128]{1,0:T(8,128)S(1)} %get-tuple-element.12.refs_2_, ...), custom_call_target="tpu_custom_call" | custom-call | tf_op jit(solution)/shard_map/finish/pallas_call | solution.py:603
